TPU v7x, 32 devices: a whole 2x2x4 slice. The times are simulated.
32 devices in a mesh: pipe: 2 (over y), tensor: 2 (over core), dp: 8 (over z, x).
Axes of the slice: x: 2, y: 2, z: 4, core: 2. Of those that a mesh axis runs over, the one named last changes fastest.
Arguments:
- images_in: bfloat16 [2, 8, 200, 768], P(None, 'dp', 'tensor'), may hold values from -6 to 6
- out_grad: bfloat16 [2, 8, 200, 768], P(None, 'dp', 'tensor'), may hold values from -6 to 6
- attn_gain: bfloat16 [2, 768], P('pipe', 'dp'), may hold values from 0.5 to 1.5
- attn_bias: bfloat16 [2, 768], P('pipe', 'dp'), may hold values from -3 to 3
- qkv_weight: bfloat16 [2, 3, 768, 768], P('pipe', None, 'dp', 'tensor'), may hold values from -0.3125 to 0.3125
- proj_weight: bfloat16 [2, 768, 768], P('pipe', 'tensor', 'dp'), may hold values from -0.3125 to 0.3125
- moe_gain: bfloat16 [2, 768], P('pipe', 'dp'), may hold values from 0.5 to 1.5
- moe_bias: bfloat16 [2, 768], P('pipe', 'dp'), may hold values from -3 to 3
- router_weight: bfloat16 [2, 768, 4], P('pipe', 'dp'), may hold values from -0.3125 to 0.3125
- inner_weight: bfloat16 [2, 4, 768, 3072], P('pipe', None, 'dp', 'tensor'), may hold values from -0.21875 to 0.21875
- outer_weight: bfloat16 [2, 4, 3072, 768], P('pipe', None, 'tensor', 'dp'), may hold values from -0.3125 to 0.3125
- expert_ids: int32 [2, 2, 8, 200, 2], P('pipe', None, 'dp'), may hold values from 0 to 3, as said below
- slot_ids: int32 [2, 2, 8, 200, 2], P('pipe', None, 'dp'), may hold values from 0 to 128, as said below
Outputs:
- activations: bfloat16 [2, 2, 8, 200, 768], P('pipe', None, 'dp', 'tensor')
- input_grads: float32 [2, 2, 8, 200, 768], P('pipe', None, 'dp', 'tensor')
- grad_attn_gain: float32 [2, 768], P('pipe', 'dp')
- grad_attn_bias: float32 [2, 768], P('pipe', 'dp')
- grad_qkv_weight: float32 [2, 3, 768, 768], P('pipe', None, 'dp', 'tensor')
- grad_proj_weight: float32 [2, 768, 768], P('pipe', 'tensor', 'dp')
- grad_moe_gain: float32 [2, 768], P('pipe', 'dp')
- grad_moe_bias: float32 [2, 768], P('pipe', 'dp')
- grad_router_weight: float32 [2, 768, 4], P('pipe', 'dp')
- grad_inner_weight: float32 [2, 4, 768, 3072], P('pipe', None, 'dp', 'tensor')
- grad_outer_weight: float32 [2, 4, 3072, 768], P('pipe', None, 'tensor', 'dp')
Inputs may be any that keep to these rules, and one draw needn't show every extreme that they name: `expert_ids`: each token's two choices name different experts; in every image some expert is the first choice of 129 or more live tokens. `slot_ids`: A choice's slot is its rank among the image's choices of that expert by live tokens, all first choices in token order before all second choices; 128 marks a choice of rank 128 or more, or of a padding position. In every image some expert fills all 128 slots.
All inputs are finite; a program needn't handle non-finite values.
Results may differ from a plain program's by a relative error of at most 0.028.
Values may be sent and summed in bfloat16 or wider, within the bound.
A program may use at most 256 MiB of HBM per device.

v0:
```python
from functools import partial

import jax
import jax.numpy as jnp
from jax import lax
from jax.sharding import PartitionSpec as P

HEAD_DIM = 64
LIVE = 197
CAP = 128


epsilon = 1e-06


def from_behind(value, axis, steps):
    count = lax.axis_size(axis)
    leading, last = (max(0, -steps), min(count, count - steps))
    return lax.ppermute(value, axis, [(source, source + steps) for source in range(leading, last)])


def layer_norm(values, norm_gain, norm_bias):
    centre = values - jnp.mean(values, axis=-1, keepdims=True)
    spread = jnp.mean(centre * centre, axis=-1, keepdims=True)
    return centre * lax.rsqrt(spread + epsilon) * norm_gain + norm_bias


def gather_rows(values):
    return lax.all_gather(values, "tensor", axis=1, tiled=True)


def scatter_rows(values):
    return lax.psum_scatter(values, "tensor", scatter_dimension=1, tiled=True)


def gather_grads(values):
    return lax.all_gather(values, "tensor", axis=1, tiled=True)


def scatter_grads(values):
    return lax.psum_scatter(
        values.astype(jnp.bfloat16), "tensor", scatter_dimension=1, tiled=True
    ).astype(jnp.float32)


def routing_tables(route_now, slots_now, experts):
    columns = jnp.arange(experts * CAP, dtype=jnp.int32)
    slot_codes = jnp.where(slots_now < CAP, route_now * CAP + slots_now, -1)
    picked = slot_codes[..., None] == columns
    expert_hot = route_now[..., None] == jnp.arange(experts, dtype=jnp.int32)
    return (picked, expert_hot)


def slot_columns(route_now, slots_now):
    kept_choice = slots_now < CAP
    codes = jnp.where(kept_choice, route_now * CAP + slots_now, 0)
    return (codes, kept_choice)


def pick_rows(table, codes, kept_choice):
    images, length, choices = codes.shape
    taken = jnp.take_along_axis(table, codes.reshape(images, length * choices)[..., None], axis=1)
    taken = taken.reshape(images, length, choices, table.shape[-1])
    return jnp.where(kept_choice[..., None], taken, 0.0)


def place_rows(values, codes, kept_choice, columns):
    images, length, choices, features = values.shape
    offsets = (jnp.arange(images, dtype=jnp.int32) * columns)[:, None, None]
    flat_index = jnp.where(kept_choice, codes + offsets, images * columns).reshape(-1)
    placed = jnp.zeros((images * columns, features), jnp.float32)
    placed = placed.at[flat_index].add(values.reshape(-1, features), mode="drop")
    return placed.reshape(images, columns, features)


def attention_scores(query_rows, key_rows):
    length = key_rows.shape[1]
    score_scale = HEAD_DIM ** (-0.5)
    scores = (
        jnp.einsum("iqhd,ikhd->ihqk", query_rows, key_rows, preferred_element_type=jnp.float32)
        * score_scale
    )
    live_keys = jnp.arange(length) < LIVE
    return jnp.where(live_keys, scores, -1e30)


def forward_layer(section_input, weights, route_now, slots_now):
    (
        gain_one,
        bias_one,
        qkv_full,
        proj_full,
        gain_two,
        bias_two,
        router_full,
        inner_full,
        outer_full,
    ) = weights
    residual_in = section_input.astype(jnp.float32)
    normed_one = layer_norm(
        residual_in, gain_one.astype(jnp.float32), bias_one.astype(jnp.float32)
    ).astype(jnp.bfloat16)
    tokens_one = gather_rows(normed_one)
    images, length, features = tokens_one.shape
    heads_here = qkv_full.shape[2] // HEAD_DIM
    projected = jnp.einsum(
        "isd,jde->jise", tokens_one, qkv_full, preferred_element_type=jnp.float32
    ).astype(jnp.bfloat16)
    query_rows = projected[0].reshape(images, length, heads_here, HEAD_DIM)
    key_rows = projected[1].reshape(images, length, heads_here, HEAD_DIM)
    value_rows = projected[2].reshape(images, length, heads_here, HEAD_DIM)
    scores = attention_scores(query_rows, key_rows)
    top_score = jnp.max(scores, axis=-1, keepdims=True)
    exp_scores = jnp.exp(scores - top_score)
    exp_total = jnp.sum(exp_scores, axis=-1, keepdims=True)
    attention = exp_scores / exp_total
    log_total = top_score + jnp.log(exp_total)
    attended = jnp.einsum(
        "ihqk,ikhd->iqhd",
        attention.astype(jnp.bfloat16),
        value_rows,
        preferred_element_type=jnp.float32,
    )
    attended = attended.astype(jnp.bfloat16).reshape(images, length, heads_here * HEAD_DIM)
    partial_attn = jnp.einsum(
        "ise,ed->isd", attended, proj_full, preferred_element_type=jnp.float32
    )
    hidden_res = residual_in + scatter_rows(partial_attn)
    normed_two = layer_norm(
        hidden_res, gain_two.astype(jnp.float32), bias_two.astype(jnp.float32)
    ).astype(jnp.bfloat16)
    tokens_two = gather_rows(normed_two)
    logits = jnp.einsum("isd,de->ise", tokens_two, router_full, preferred_element_type=jnp.float32)
    router_probs = jax.nn.softmax(logits, axis=-1)
    experts = router_full.shape[1]
    picked, expert_hot = routing_tables(route_now, slots_now, experts)
    codes, kept_choice = slot_columns(route_now, slots_now)
    gate_values = jnp.sum(jnp.where(expert_hot, router_probs[:, :, None, :], 0.0), axis=-1)
    dispatch = jnp.any(picked, axis=2).astype(jnp.bfloat16)
    expert_rows = jnp.einsum(
        "isc,isd->icd", dispatch, tokens_two, preferred_element_type=jnp.float32
    ).astype(jnp.bfloat16)
    expert_rows = expert_rows.reshape(images, experts, CAP, features)
    pre_act = jnp.einsum(
        "iecd,edf->iecf", expert_rows, inner_full, preferred_element_type=jnp.float32
    )
    activated = jax.nn.gelu(pre_act, approximate=True).astype(jnp.bfloat16)
    expert_out = jnp.einsum(
        "iecf,efd->iecd", activated, outer_full, preferred_element_type=jnp.float32
    )
    expert_out = expert_out.reshape(images, experts * CAP, features)
    chosen_out = pick_rows(expert_out, codes, kept_choice)
    partial_moe = jnp.sum(chosen_out * gate_values[..., None], axis=2)
    section_output = hidden_res + scatter_rows(partial_moe)
    kept_values = (
        residual_in,
        hidden_res,
        tokens_one,
        query_rows,
        key_rows,
        value_rows,
        log_total,
        attended,
        tokens_two,
        router_probs,
        gate_values,
        expert_rows,
        pre_act,
        activated,
        expert_out,
    )
    return (section_output, kept_values)


def backward_layer(cotangent, kept_values, weights, route_now, slots_now):
    (
        gain_one,
        bias_one,
        qkv_full,
        proj_full,
        gain_two,
        bias_two,
        router_full,
        inner_full,
        outer_full,
    ) = weights
    (
        residual_in,
        hidden_res,
        tokens_one,
        query_rows,
        key_rows,
        value_rows,
        log_total,
        attended,
        tokens_two,
        router_probs,
        gate_values,
        expert_rows,
        pre_act,
        activated,
        expert_out,
    ) = kept_values
    images, length, features = tokens_one.shape
    heads_here = qkv_full.shape[2] // HEAD_DIM
    experts = router_full.shape[1]
    score_scale = HEAD_DIM ** (-0.5)
    picked, expert_hot = routing_tables(route_now, slots_now, experts)
    codes, kept_choice = slot_columns(route_now, slots_now)
    grad_out = cotangent.astype(jnp.float32)
    grad_full = gather_grads(cotangent).astype(jnp.float32)
    weighted = gate_values[..., None] * grad_full[:, :, None, :]
    grad_expert = place_rows(weighted, codes, kept_choice, experts * CAP).astype(jnp.bfloat16)
    chosen_out = pick_rows(expert_out, codes, kept_choice)
    grad_gates = jnp.sum(grad_full[:, :, None, :] * chosen_out, axis=-1)
    grad_probs = jnp.sum(jnp.where(expert_hot, grad_gates[..., None], 0.0), axis=2)
    grad_logits = router_probs * (
        grad_probs - jnp.sum(router_probs * grad_probs, axis=-1, keepdims=True)
    )
    grad_router = jnp.einsum(
        "isd,ise->de", tokens_two.astype(jnp.float32), grad_logits, precision=lax.Precision.HIGHEST
    )
    grad_tokens_two = jnp.einsum(
        "ise,de->isd", grad_logits, router_full.astype(jnp.float32), precision=lax.Precision.HIGHEST
    )
    grad_blocks = grad_expert.reshape(images, experts, CAP, features)
    grad_outer = jnp.einsum(
        "iecf,iecd->efd", activated, grad_blocks, preferred_element_type=jnp.float32
    )
    grad_act = jnp.einsum(
        "iecd,efd->iecf", grad_blocks, outer_full, preferred_element_type=jnp.float32
    )
    gelu_pull = jax.vjp(partial(jax.nn.gelu, approximate=True), pre_act)[1]
    grad_pre = gelu_pull(grad_act)[0].astype(jnp.bfloat16)
    grad_inner = jnp.einsum(
        "iecd,iecf->edf", expert_rows, grad_pre, preferred_element_type=jnp.float32
    )
    grad_rows = jnp.einsum(
        "iecf,edf->iecd", grad_pre, inner_full, preferred_element_type=jnp.float32
    )
    grad_rows = grad_rows.reshape(images, experts * CAP, features)
    grad_tokens_two = grad_tokens_two + jnp.sum(pick_rows(grad_rows, codes, kept_choice), axis=2)
    grad_normed_two = scatter_grads(grad_tokens_two)
    norm_two_pull = jax.vjp(
        layer_norm, hidden_res, gain_two.astype(jnp.float32), bias_two.astype(jnp.float32)
    )[1]
    grad_hidden_ln, grad_gain_two, grad_bias_two = norm_two_pull(grad_normed_two)
    grad_hidden = grad_out + grad_hidden_ln
    grad_branch = gather_grads(grad_hidden.astype(jnp.bfloat16))
    grad_proj = jnp.einsum("ise,isd->ed", attended, grad_branch, preferred_element_type=jnp.float32)
    grad_attended = jnp.einsum(
        "isd,ed->ise", grad_branch, proj_full, preferred_element_type=jnp.float32
    )
    grad_attended = grad_attended.astype(jnp.bfloat16).reshape(images, length, heads_here, HEAD_DIM)
    attention = jnp.exp(attention_scores(query_rows, key_rows) - log_total)
    grad_values = jnp.einsum(
        "ihqk,iqhd->ikhd",
        attention.astype(jnp.bfloat16),
        grad_attended,
        preferred_element_type=jnp.float32,
    ).astype(jnp.bfloat16)
    grad_weights_att = jnp.einsum(
        "iqhd,ikhd->ihqk", grad_attended, value_rows, preferred_element_type=jnp.float32
    )
    grad_scores = attention * (
        grad_weights_att - jnp.sum(attention * grad_weights_att, axis=-1, keepdims=True)
    )
    grad_scores = grad_scores.astype(jnp.bfloat16)
    grad_queries = (
        jnp.einsum("ihqk,ikhd->iqhd", grad_scores, key_rows, preferred_element_type=jnp.float32)
        * score_scale
    ).astype(jnp.bfloat16)
    grad_keys = (
        jnp.einsum("ihqk,iqhd->ikhd", grad_scores, query_rows, preferred_element_type=jnp.float32)
        * score_scale
    ).astype(jnp.bfloat16)
    grad_projected = jnp.stack([grad_queries, grad_keys, grad_values]).reshape(
        3, images, length, heads_here * HEAD_DIM
    )
    grad_qkv = jnp.einsum(
        "isd,jise->jde", tokens_one, grad_projected, preferred_element_type=jnp.float32
    )
    grad_tokens_one = jnp.einsum(
        "jise,jde->isd", grad_projected, qkv_full, preferred_element_type=jnp.float32
    )
    grad_normed_one = scatter_grads(grad_tokens_one)
    norm_one_pull = jax.vjp(
        layer_norm, residual_in, gain_one.astype(jnp.float32), bias_one.astype(jnp.float32)
    )[1]
    grad_input_ln, grad_gain_one, grad_bias_one = norm_one_pull(grad_normed_one)
    grad_input = grad_hidden + grad_input_ln
    return (
        grad_input,
        (
            grad_gain_one,
            grad_bias_one,
            grad_qkv,
            grad_proj,
            grad_gain_two,
            grad_bias_two,
            grad_router,
            grad_inner,
            grad_outer,
        ),
    )


def pick_section(is_first, early_part, late_part):
    return jax.tree.map(
        lambda early_leaf, late_leaf: jnp.where(is_first, early_leaf, late_leaf),
        early_part,
        late_part,
    )


def body(
    images_in,
    out_grad,
    attn_gain,
    attn_bias,
    qkv_weight,
    proj_weight,
    moe_gain,
    moe_bias,
    router_weight,
    inner_weight,
    outer_weight,
    expert_ids,
    slot_ids,
):
    section_index = lax.axis_index("pipe")
    is_first = section_index == 0
    micro_count = images_in.shape[0]
    gathered = (
        lax.all_gather(attn_gain, "dp", axis=1, tiled=True),
        lax.all_gather(attn_bias, "dp", axis=1, tiled=True),
        lax.all_gather(qkv_weight, "dp", axis=2, tiled=True),
        lax.all_gather(proj_weight, "dp", axis=2, tiled=True),
        lax.all_gather(moe_gain, "dp", axis=1, tiled=True),
        lax.all_gather(moe_bias, "dp", axis=1, tiled=True),
        lax.all_gather(router_weight, "dp", axis=1, tiled=True),
        lax.all_gather(inner_weight, "dp", axis=2, tiled=True),
        lax.all_gather(outer_weight, "dp", axis=3, tiled=True),
    )
    weights = tuple((member[0] for member in gathered))
    routes = expert_ids[0]
    slots_all = slot_ids[0]
    received = jnp.zeros(images_in.shape[1:], jnp.bfloat16)
    outputs = []
    saved_ticks = []
    for tick_step in range(micro_count + 1):
        first_mb = min(tick_step, micro_count - 1)
        later_mb = max(tick_step - 1, 0)
        section_input = jnp.where(is_first, images_in[first_mb], received)
        route_now = jnp.where(is_first, routes[first_mb], routes[later_mb])
        slots_now = jnp.where(is_first, slots_all[first_mb], slots_all[later_mb])
        result, kept_values = forward_layer(section_input, weights, route_now, slots_now)
        result_low = result.astype(jnp.bfloat16)
        outputs.append(result_low)
        saved_ticks.append((kept_values, route_now, slots_now))
        if tick_step < micro_count:
            received = from_behind(result_low, "pipe", 1)
    activations = jnp.stack(
        [
            jnp.where(is_first, outputs[mb_index], outputs[mb_index + 1])
            for mb_index in range(micro_count)
        ]
    )[None]
    regathered = (
        lax.all_gather(attn_gain, "dp", axis=1, tiled=True),
        lax.all_gather(attn_bias, "dp", axis=1, tiled=True),
        lax.all_gather(qkv_weight, "dp", axis=2, tiled=True),
        lax.all_gather(proj_weight, "dp", axis=2, tiled=True),
        lax.all_gather(moe_gain, "dp", axis=1, tiled=True),
        lax.all_gather(moe_bias, "dp", axis=1, tiled=True),
        lax.all_gather(router_weight, "dp", axis=1, tiled=True),
        lax.all_gather(inner_weight, "dp", axis=2, tiled=True),
        lax.all_gather(outer_weight, "dp", axis=3, tiled=True),
    )
    back_weights = tuple((member[0] for member in regathered))
    received_grad = jnp.zeros(out_grad.shape[1:], jnp.bfloat16)
    totals = None
    input_list = []
    for tick_step in range(micro_count + 1):
        early_mb = max(tick_step - 1, 0)
        late_mb = min(tick_step, micro_count - 1)
        cotangent = jnp.where(is_first, received_grad, out_grad[late_mb])
        if tick_step == micro_count:
            cotangent = jnp.where(is_first, cotangent, jnp.zeros_like(cotangent))
        kept_pair = pick_section(is_first, saved_ticks[early_mb], saved_ticks[late_mb + 1])
        kept_now, route_now, slots_now = kept_pair
        grad_input, grad_terms = backward_layer(
            cotangent, kept_now, back_weights, route_now, slots_now
        )
        totals = grad_terms if totals is None else jax.tree.map(jnp.add, totals, grad_terms)
        input_list.append(grad_input)
        if tick_step < micro_count:
            received_grad = from_behind(grad_input.astype(jnp.bfloat16), "pipe", -1)
    input_grads = jnp.stack(
        [
            jnp.where(is_first, input_list[mb_index + 1], input_list[mb_index])
            for mb_index in range(micro_count)
        ]
    )[None]
    small_local = (totals[0], totals[1], totals[4], totals[5], totals[6])
    small_sums = lax.psum(
        (small_local[0], small_local[1], small_local[2], small_local[3], small_local[4]), "tensor"
    )
    shards = (
        lax.psum_scatter(
            small_sums[0][None].astype(jnp.bfloat16), "dp", scatter_dimension=1, tiled=True
        ).astype(jnp.float32),
        lax.psum_scatter(
            small_sums[1][None].astype(jnp.bfloat16), "dp", scatter_dimension=1, tiled=True
        ).astype(jnp.float32),
        lax.psum_scatter(
            totals[2][None].astype(jnp.bfloat16), "dp", scatter_dimension=2, tiled=True
        ).astype(jnp.float32),
        lax.psum_scatter(
            totals[3][None].astype(jnp.bfloat16), "dp", scatter_dimension=2, tiled=True
        ).astype(jnp.float32),
        lax.psum_scatter(
            small_sums[2][None].astype(jnp.bfloat16), "dp", scatter_dimension=1, tiled=True
        ).astype(jnp.float32),
        lax.psum_scatter(
            small_sums[3][None].astype(jnp.bfloat16), "dp", scatter_dimension=1, tiled=True
        ).astype(jnp.float32),
        lax.psum_scatter(
            small_sums[4][None].astype(jnp.bfloat16), "dp", scatter_dimension=1, tiled=True
        ).astype(jnp.float32),
        lax.psum_scatter(
            totals[7][None].astype(jnp.bfloat16), "dp", scatter_dimension=2, tiled=True
        ).astype(jnp.float32),
        lax.psum_scatter(
            totals[8][None].astype(jnp.bfloat16), "dp", scatter_dimension=3, tiled=True
        ).astype(jnp.float32),
    )
    return (
        activations,
        input_grads,
        shards[0],
        shards[1],
        shards[2],
        shards[3],
        shards[4],
        shards[5],
        shards[6],
        shards[7],
        shards[8],
    )


def solution(mesh):
    in_specs = (
        P(None, "dp", "tensor", None),
        P(None, "dp", "tensor", None),
        P("pipe", "dp"),
        P("pipe", "dp"),
        P("pipe", None, "dp", "tensor"),
        P("pipe", "tensor", "dp"),
        P("pipe", "dp"),
        P("pipe", "dp"),
        P("pipe", "dp", None),
        P("pipe", None, "dp", "tensor"),
        P("pipe", None, "tensor", "dp"),
        P("pipe", None, "dp", None, None),
        P("pipe", None, "dp", None, None),
    )
    out_specs = (
        P("pipe", None, "dp", "tensor", None),
        P("pipe", None, "dp", "tensor", None),
        P("pipe", "dp"),
        P("pipe", "dp"),
        P("pipe", None, "dp", "tensor"),
        P("pipe", "tensor", "dp"),
        P("pipe", "dp"),
        P("pipe", "dp"),
        P("pipe", "dp", None),
        P("pipe", None, "dp", "tensor"),
        P("pipe", None, "tensor", "dp"),
    )
    return jax.shard_map(body, mesh=mesh, in_specs=in_specs, out_specs=out_specs, check_vma=False)
```

profile of v0, /device:TPU:0, one launch (start us, length us, event | category | flops | bytes accessed | tf_op | source)
XLA Modules:
  0.0 1785.8 jit_solution(8573915427229598333)
XLA Ops:
  13.3 23.5 %all-reduce.24 = (bf16[768]{0:T(1024)(128)(2,1)S(1)}, bf16[768]{0:T(1024)(128)(2,1)S(1)}, bf16[768]{0:T(1024)(128)(2,1)S(1)}, bf16[768]{0:T(1024)(128)(2,1)S(1)}) all-reduce(bf16[768]{0:T(1024)(128)(2,1)S(1)} %dynamic-update-slice.1, bf16[768]{0:T(1024)(128)(2,1)S(1)} %dynamic-update-slice, ...), channel_id=1, replica_groups=mesh['pipe'=2,'tensor'=2,'dp'=8] {'dp'}, use_global_device_ids=true, to_apply=%add.1 | all-reduce | flops 3072 | bytes 12288
  44.0 32.5 %all_gather.74 = bf16[1,384,768]{1,2,0:T(8,128)(2,1)S(1)} all-gather(bf16[1,384,96]{1,2,0:T(8,128)(2,1)S(1)} %copy-done.153), channel_id=1, replica_groups=mesh['pipe'=2,'tensor'=2,'dp'=8] {'dp'}, dimensions={2}, use_global_device_ids=true | all-gather | bytes 663552 | tf_op jit(solution)/shard_map/all_gather | solution.py:338
  88.7 31.6 %all_gather.80 = bf16[1,768,4]{2,0,1:T(2,128)(2,1)S(1)} all-gather(bf16[1,96,4]{2,0,1:T(2,128)(2,1)S(1)} %copy.465), channel_id=1, replica_groups=mesh['pipe'=2,'tensor'=2,'dp'=8] {'dp'}, dimensions={1}, use_global_device_ids=true | all-gather | bytes 6912 | tf_op jit(solution)/shard_map/all_gather | solution.py:341
  129.1 112.0 %all-gather.9.cloned.1.call-done = bf16[1,4,1536,768]{2,1,0,3:T(4,128)(2,1)} async-done(((bf16[1,4,1536,96]{2,1,0,3:T(4,128)(2,1)}), bf16[1,4,1536,768]{2,1,0,3:T(4,128)(2,1)}) %all-gather.9.cloned.1.call-update) | async-done | bytes 9437200 | tf_op jit(solution)/shard_map/all_gather | solution.py:343
  241.2 15.6 copy.464
  256.8 122.7 %all-gather.7.cloned.1.call-done = bf16[1,4,768,1536]{3,2,1,0:T(8,128)(2,1)} async-done(((bf16[1,4,96,1536]{3,2,1,0:T(8,128)(2,1)}), bf16[1,4,768,1536]{3,2,1,0:T(8,128)(2,1)}) %all-gather.7.cloned.1.call-update) | async-done | bytes 9437200 | tf_op jit(solution)/shard_map/all_gather | solution.py:342
  403.1 14.4 all-reduce.35.cloned.1.call-done
  451.4 10.5 all-reduce.37.cloned.1.call-done
  474.3 6.7 fusion.16
  521.3 10.8 fusion.107
  589.1 18.3 %all-reduce.41.cloned.1.call-done = f32[1,200,768]{2,0,1:T(1,128)} async-done(((f32[1,200,768]{2,0,1:T(1,128)}), f32[1,200,768]{2,0,1:T(1,128)}) %all-reduce.41.cloned.1.call-update) | async-done | bytes 614416
  607.4 6.9 multiply_reduce_fusion.20
  661.2 6.7 fusion.14
  681.5 7.0 collective-permute-done.2
  704.7 10.7 fusion.104
  763.7 8.9 collective-permute-done.3
  784.5 10.7 fusion.101
  863.1 11.7 fusion.125
  874.8 8.1 fusion.123
  883.0 17.3 fusion.7
  900.3 16.6 copy.566
  918.8 9.5 fusion.235
  928.7 10.8 fusion.233
  939.5 17.1 fusion.6
  964.5 62.1 %reduce-scatter.51.cloned.1.call-done = bf16[96,1]{1,0:T(8,128)(2,1)} async-done(((bf16[768,1]{1,0:T(8,128)(2,1)}), bf16[96,1]{1,0:T(8,128)(2,1)}) %reduce-scatter.51.cloned.1.call-update) | async-done | bytes 208
  1027.9 61.9 %reduce-scatter.53.cloned.1.call-done = bf16[96,1]{1,0:T(8,128)(2,1)} async-done(((bf16[768,1]{1,0:T(8,128)(2,1)}), bf16[96,1]{1,0:T(8,128)(2,1)}) %reduce-scatter.53.cloned.1.call-update) | async-done | bytes 208
  1091.1 62.0 %reduce-scatter.55.cloned.1.call-done = bf16[96,4]{1,0:T(8,128)(2,1)} async-done(((bf16[768,4]{1,0:T(8,128)(2,1)}), bf16[96,4]{1,0:T(8,128)(2,1)}) %reduce-scatter.55.cloned.1.call-update) | async-done | bytes 784
  1154.6 18.7 %all-reduce.43.cloned.1.call-done = f32[1,200,768]{2,0,1:T(1,128)} async-done(((f32[1,200,768]{2,0,1:T(1,128)}), f32[1,200,768]{2,0,1:T(1,128)}) %all-reduce.43.cloned.1.call-update) | async-done | bytes 614416
  1175.9 63.9 %reduce-scatter.49.cloned.1.call-done = bf16[96,384]{1,0:T(8,128)(2,1)} async-done(((bf16[768,384]{1,0:T(8,128)(2,1)}), bf16[96,384]{1,0:T(8,128)(2,1)}) %reduce-scatter.49.cloned.1.call-update) | async-done | bytes 73744
  1241.7 67.4 %reduce-scatter.47.cloned.1.call-done = bf16[96,1152]{1,0:T(8,128)(2,1)} async-done(((bf16[768,1152]{1,0:T(8,128)(2,1)}), bf16[96,1152]{1,0:T(8,128)(2,1)}) %reduce-scatter.47.cloned.1.call-update) | async-done | bytes 221200
  1311.3 298.5 %all-reduce.45.cloned.1.call-done = bf16[1,4,1536,768]{2,1,0,3:T(4,128)(2,1)} async-done(((bf16[1,4,1536,768]{2,1,0,3:T(4,128)(2,1)}), bf16[1,4,1536,768]{2,1,0,3:T(4,128)(2,1)}) %all-reduce.45.cloned.1.call-update) | async-done | bytes 9437200
  1613.6 162.2 %reduce-scatter.41.cloned.1.call-done = bf16[1,4,96,1536]{3,2,1,0:T(8,128)(2,1)} async-done(((bf16[1,4,768,1536]{3,2,1,0:T(8,128)(2,1)}), bf16[1,4,96,1536]{3,2,1,0:T(8,128)(2,1)}) %reduce-scatter.41.cloned.1.call-update) | async-done | bytes 1179664 | tf_op jit(solution)/shard_map/reduce_scatter | solution.py:431
  (915 shorter events, 427.6 us)
Async XLA Ops:
  7.2 69.3 %all-gather.5.cloned.1.call-start = ((), (), s32[]{:S(2)}) async-start(), calls=%async_computation.8 | async-start | bytes 1990656 | tf_op jit(solution)/shard_map/all_gather | solution.py:337
  7.9 115.3 %all-reduce.33.cloned.1.call-start = ((), (), s32[]{:S(2)}) async-start(), calls=%async_computation.19 | async-start | bytes 1228800
  36.8 392.7 %copy-start.156 = (f32[768]{0:T(1024)}, f32[768]{0:T(1024)S(1)}, u32[]{:S(2)}) copy-start(f32[768]{0:T(1024)S(1)} %convert_element_type.686) | copy-start | bytes 9220
  44.0 392.3 %copy-start.176 = (pred[200]{0:T(512)(128)(4,1)}, pred[200]{0:T(512)(128)(4,1)S(1)}, u32[]{:S(2)}) copy-start(pred[200]{0:T(512)(128)(4,1)S(1)} %iota_compare_fusion.9) | copy-start | bytes 604
  82.4 158.7 %all-gather.9.cloned.1.call-start = ((), (), s32[]{:S(2)}) async-start(), calls=%async_computation.10 | async-start | bytes 10616832 | tf_op jit(solution)/shard_map/all_gather | solution.py:343
  84.4 295.0 %all-gather.7.cloned.1.call-start = ((), (), s32[]{:S(2)}) async-start(), calls=%async_computation.9 | async-start | bytes 10616832 | tf_op jit(solution)/shard_map/all_gather | solution.py:342
  85.0 332.5 %all-reduce.35.cloned.1.call-start = ((), (), s32[]{:S(2)}) async-start(), calls=%async_computation.20 | async-start | bytes 1228800
  120.6 428.8 %copy-start.136 = (bf16[1,768,4]{1,2,0:T(4,128)(2,1)}, bf16[1,768,4]{1,2,0:T(4,128)(2,1)S(1)}, u32[]{:S(2)}) copy-start(bf16[1,768,4]{1,2,0:T(4,128)(2,1)S(1)} %copy.466) | copy-start | bytes 18436
  127.7 436.4 %copy-start.147 = (f32[200]{0:T(256)}, f32[200]{0:T(256)S(1)}, u32[]{:S(2)}) copy-start(f32[200]{0:T(256)S(1)} %get-tuple-element.236) | copy-start | bytes 2404
  400.3 61.6 %all-reduce.37.cloned.1.call-start = ((), (), s32[]{:S(2)}) async-start(), calls=%async_computation.21 | async-start | bytes 1228800
  419.2 7.8 collective-permute-start
  440.1 118.0 %all-reduce.39.cloned.1.call-start = ((), (), s32[]{:S(2)}) async-start(), calls=%async_computation.22 | async-start | bytes 1228800
  514.0 93.4 %all-reduce.41.cloned.1.call-start = ((), (), s32[]{:S(2)}) async-start(), calls=%async_computation.23 | async-start | bytes 1228800
  555.9 9.1 collective-permute-start.4
  561.3 7.6 collective-permute-start.1
  588.4 373.4 %reduce-scatter.43.cloned.1.call-start = ((), (), s32[]{:S(2)}) async-start(), calls=%async_computation.12 | async-start | bytes 221184
  653.6 16.6 collective-permute-start.5
  677.7 10.8 collective-permute-start.2
  728.6 3.1 collective-permute-start.6
  749.1 8.0 collective-permute-start.7
  762.1 10.5 collective-permute-start.3
  809.8 3.1 collective-permute-start.8
  829.3 2.9 collective-permute-start.9
  838.3 124.8 %reduce-scatter.45.cloned.1.call-start = ((), (), s32[]{:S(2)}) async-start(), calls=%async_computation.13 | async-start | bytes 221184
  839.2 187.3 %reduce-scatter.51.cloned.1.call-start = ((), (), s32[]{:S(2)}) async-start(), calls=%async_computation.16 | async-start | bytes 221184
  840.2 249.6 %reduce-scatter.53.cloned.1.call-start = ((), (), s32[]{:S(2)}) async-start(), calls=%async_computation.17 | async-start | bytes 221184
  841.1 312.1 %reduce-scatter.55.cloned.1.call-start = ((), (), s32[]{:S(2)}) async-start(), calls=%async_computation.18 | async-start | bytes 221184
  843.4 330.0 %all-reduce.43.cloned.1.call-start = ((), (), s32[]{:S(2)}) async-start(), calls=%async_computation.24 | async-start | bytes 1228800
  847.2 392.6 %reduce-scatter.49.cloned.1.call-start = ((), (), s32[]{:S(2)}) async-start(), calls=%async_computation.15 | async-start | bytes 663552
  852.2 456.9 %reduce-scatter.47.cloned.1.call-start = ((), (), s32[]{:S(2)}) async-start(), calls=%async_computation.14 | async-start | bytes 1990656
  863.0 746.8 %all-reduce.45.cloned.1.call-start = ((), (), s32[]{:S(2)}) async-start(), calls=%async_computation.25 | async-start | bytes 18874368
  916.9 858.9 %reduce-scatter.41.cloned.1.call-start = ((), (), s32[]{:S(2)}) async-start(), calls=%async_computation.11 | async-start | bytes 10616832 | tf_op jit(solution)/shard_map/reduce_scatter | solution.py:431
  (223 other events, 3354.7 us)
Sparse Core Ops, SparseCore 0:
  10.2 55.2 all-gather.4
  82.5 16.2 all-reduce.32
  101.6 139.4 all-gather.8
  243.2 136.2 all-gather.6
  400.4 17.0 all-reduce.34
  440.2 21.6 all-reduce.36
  514.2 19.4 all-reduce.38
  588.5 18.8 all-reduce.40
  838.4 61.3 reduce-scatter.42
  902.9 60.1 reduce-scatter.44
  966.4 60.1 reduce-scatter.50
  1029.7 60.0 reduce-scatter.52
  1093.0 60.0 reduce-scatter.54
  1155.4 17.9 all-reduce.42
  1176.5 63.2 reduce-scatter.48
  1244.1 64.9 reduce-scatter.46
  1312.8 297.0 all-reduce.44
  1613.3 162.4 reduce-scatter.40
where the time goes:
time: 1800 us; the launch traced here: 1790 us
  waiting for transfers between devices  1090 us (61%)
  matrix products  186 us (10%)
  local copies, waits for them, and re-layouts  180 us (10%)
  blocking collectives  142 us (8%)
  other arithmetic  139 us (8%)
  starting transfers between devices  23.8 us (1%)
  between operations  20.9 us (1%)
    unnamed x38, waiting for transfers between devices  681 us
    reduce_scatter x1, waiting for transfers between devices, body(): lax.psum_scatter(totals[7][None].astype(jnp.bfloat16), 'dp', scatter_dime...  162 us
    all_gather x1, waiting for transfers between devices, body(): lax.all_gather(inner_weight, 'dp', axis=2, tiled=True)  123 us
    all_gather x1, waiting for transfers between devices, body(): lax.all_gather(outer_weight, 'dp', axis=3, tiled=True)  112 us
    unnamed x517, local copies, waits for them, and re-layouts  54.9 us
    unnamed x7, blocking collectives  45.7 us
    dot_general x3, matrix products, backward_layer(): jnp.einsum('iecd,iecf->edf', expert_rows, grad_pre, preferred_element_typ...  37.4 us
    dot_general x3, matrix products, backward_layer(): jnp.einsum('iecf,iecd->efd', activated, grad_blocks, preferred_element_ty...  37.1 us
  transfers between devices with their start and end apart: 28, of which 18 were waited for; matrix products, arithmetic and copies ran while one was open for 14% of the time, Pallas kernels for 0%

commit v1 on v0

v1 whole, which is shorter than its diff:
```python
import jax
import jax.numpy as jnp
from jax import lax
from jax.sharding import PartitionSpec as P

HEAD_DIM = 64
LIVE = 197
CAP = 128
ROWS = 128
EPS = 1e-06
BF = jnp.bfloat16
F32 = jnp.float32


def dot(spec, left, right):
    return jnp.einsum(spec, left, right, preferred_element_type=F32)


def swap(values):
    return lax.ppermute(values, "tensor", [(0, 1), (1, 0)])


def join_halves(own):
    return jnp.concatenate([own, swap(own)], axis=1)


def sum_halves(full, wire):
    rows = full.shape[1] // 2
    return full[:, :rows].astype(F32) + swap(full[:, rows:].astype(wire)).astype(F32)


def norm_stats(values):
    centre = values - jnp.mean(values, axis=-1, keepdims=True)
    inv = lax.rsqrt(jnp.mean(centre * centre, axis=-1, keepdims=True) + EPS)
    return centre * inv, inv


def norm_back(grad, unit, inv, gain):
    scaled = grad * gain
    return (
        scaled
        - jnp.mean(scaled, axis=-1, keepdims=True)
        - unit * jnp.mean(scaled * unit, axis=-1, keepdims=True)
    ) * inv


def gelu_parts(pre):
    inner = 0.7978845608028654 * (pre + 0.044715 * pre * pre * pre)
    return jnp.tanh(inner)


def forward(section_input, weights, tables):
    gain1, bias1, gain2, bias2, qkv, projt, router, inner, outert = weights
    onehot, kept, hot, key_live, = tables
    images, rows, features = section_input.shape
    length = 2 * rows
    experts = router.shape[1]
    heads = qkv.shape[2] // HEAD_DIM
    z = section_input.astype(F32)
    unit1, inv1 = norm_stats(z)
    a1 = join_halves((unit1 * gain1 + bias1).astype(BF))
    qkv_rows = dot("isd,jde->jise", a1, qkv).astype(BF)
    q, k, v = (qkv_rows[j].reshape(images, length, heads, HEAD_DIM) for j in range(3))
    scores = dot("iqhd,ikhd->ihqk", q, k) * HEAD_DIM**-0.5
    scores = jnp.where(key_live, scores, -1e30)
    top = jnp.max(scores, axis=-1, keepdims=True)
    weights_exp = jnp.exp(scores - top)
    probs = weights_exp / jnp.sum(weights_exp, axis=-1, keepdims=True)
    attended = dot("ihqk,ikhd->iqhd", probs.astype(BF), v).astype(BF)
    attended = attended.reshape(images, length, heads * HEAD_DIM)
    h1 = z + sum_halves(dot("ise,de->isd", attended, projt), F32)
    unit2, inv2 = norm_stats(h1)
    a2 = join_halves((unit2 * gain2 + bias2).astype(BF))
    router_probs = jax.nn.softmax(dot("isd,de->ise", a2, router), axis=-1)
    gate = jnp.sum(jnp.where(hot, router_probs[:, None], 0.0), axis=-1)
    dispatch = onehot[:, 0] + onehot[:, 1]
    rows_e = dot("isc,isd->icd", dispatch, a2).astype(BF)
    rows_e = rows_e.reshape(images, experts, CAP, features).transpose(1, 0, 2, 3)
    rows_e = rows_e.reshape(experts, images * CAP, features)
    pre = dot("ecd,edf->ecf", rows_e, inner)
    act = (0.5 * pre * (1.0 + gelu_parts(pre))).astype(BF)
    out = dot("ecf,edf->ecd", act, outert).astype(BF)
    out = out.reshape(experts, images, CAP, features).transpose(1, 0, 2, 3)
    out = out.reshape(images, experts * CAP, features)
    chosen = dot("iksc,icd->iksd", onehot, out)
    moe = jnp.sum(chosen * gate[..., None], axis=1)
    y = h1 + sum_halves(moe, F32)
    saved = (unit1, inv1, a1, q, k, v, probs, attended, unit2, inv2, a2, router_probs, gate,
             rows_e, pre, act, chosen.astype(BF))
    return y.astype(BF), saved


def backward(dy, saved, weights, tables):
    gain1, bias1, gain2, bias2, qkv, projt, router, inner, outert = weights
    onehot, kept, hot, key_live, = tables
    (unit1, inv1, a1, q, k, v, probs, attended, unit2, inv2, a2, router_probs, gate,
     rows_e, pre, act, chosen) = saved
    images, rows, features = dy.shape
    length = 2 * rows
    experts = router.shape[1]
    heads = qkv.shape[2] // HEAD_DIM
    scale = HEAD_DIM**-0.5
    grad_full = join_halves(dy).astype(F32)
    weighted = (gate[..., None] * grad_full[:, None]).astype(BF)
    dexp = dot("iksc,iksd->icd", onehot, weighted).astype(BF)
    dexp = dexp.reshape(images, experts, CAP, features).transpose(1, 0, 2, 3)
    dexp = dexp.reshape(experts, images * CAP, features)
    grad_outert = dot("ecd,ecf->edf", dexp, act).astype(BF)
    grad_act = dot("ecd,edf->ecf", dexp, outert)
    tanh = gelu_parts(pre)
    slope = 0.5 * (1.0 + tanh) + 0.5 * pre * (1.0 - tanh * tanh) * (
        0.7978845608028654 * (1.0 + 3 * 0.044715 * pre * pre)
    )
    dpre = (grad_act * slope).astype(BF)
    grad_inner = dot("ecd,ecf->edf", rows_e, dpre).astype(BF)
    drows = dot("ecf,edf->ecd", dpre, inner).astype(BF)
    drows = drows.reshape(experts, images, CAP, features).transpose(1, 0, 2, 3)
    drows = drows.reshape(images, experts * CAP, features)
    dgate = jnp.where(kept, jnp.sum(grad_full[:, None] * chosen.astype(F32), axis=-1), 0.0)
    drouter = jnp.sum(jnp.where(hot, dgate[..., None], 0.0), axis=1)
    dlogit = router_probs * (drouter - jnp.sum(router_probs * drouter, axis=-1, keepdims=True))
    grad_router = jnp.einsum(
        "isd,ise->de", a2.astype(F32), dlogit, precision=lax.Precision.HIGHEST
    )
    da2 = jnp.einsum("ise,de->isd", dlogit, router.astype(F32), precision=lax.Precision.HIGHEST)
    da2 = da2 + dot("isc,icd->isd", onehot[:, 0] + onehot[:, 1], drows)
    da2 = sum_halves(da2, BF)
    grad_gain2 = jnp.sum(da2 * unit2, axis=(0, 1))
    grad_bias2 = jnp.sum(da2, axis=(0, 1))
    dh1 = dy.astype(F32) + norm_back(da2, unit2, inv2, gain2)
    dbranch = join_halves(dh1.astype(BF))
    grad_projt = dot("isd,ise->de", dbranch, attended).astype(BF)
    datt = dot("isd,de->ise", dbranch, projt).astype(BF)
    datt = datt.reshape(images, length, heads, HEAD_DIM)
    dv = dot("ihqk,iqhd->ikhd", probs.astype(BF), datt).astype(BF)
    dprobs = dot("iqhd,ikhd->ihqk", datt, v)
    dscores = probs * (dprobs - jnp.sum(probs * dprobs, axis=-1, keepdims=True))
    dscores = dscores.astype(BF)
    dq = (dot("ihqk,ikhd->iqhd", dscores, k) * scale).astype(BF)
    dk = (dot("ihqk,iqhd->ikhd", dscores, q) * scale).astype(BF)
    flat = tuple(part.reshape(images, length, heads * HEAD_DIM) for part in (dq, dk, dv))
    grad_qkv = tuple(dot("isd,ise->de", a1, part).astype(BF) for part in flat)
    da1 = sum(dot("ise,de->isd", part, qkv[j]) for j, part in enumerate(flat))
    da1 = sum_halves(da1, BF)
    grad_gain1 = jnp.sum(da1 * unit1, axis=(0, 1))
    grad_bias1 = jnp.sum(da1, axis=(0, 1))
    dz = dh1 + norm_back(da1, unit1, inv1, gain1)
    small = jnp.concatenate(
        [jnp.stack([grad_gain1, grad_bias1, grad_gain2, grad_bias2], axis=1), grad_router], axis=1
    )
    return dz, grad_qkv, grad_projt, small, grad_inner, grad_outert


def gather_dp(shard):
    return lax.all_gather(shard, "dp", axis=shard.ndim - 2, tiled=True)


def scatter_dp(full):
    return lax.psum_scatter(full, "dp", scatter_dimension=full.ndim - 2, tiled=True)


def body(
    images_in,
    out_grad,
    attn_gain,
    attn_bias,
    qkv_weight,
    proj_weight,
    moe_gain,
    moe_bias,
    router_weight,
    inner_weight,
    outer_weight,
    expert_ids,
    slot_ids,
):
    is_first = lax.axis_index("pipe") == 0
    side = lax.axis_index("tensor")
    micro, local, piece, features = images_in.shape
    images = micro * local
    shard, wide = qkv_weight.shape[2], qkv_weight.shape[3]
    experts = router_weight.shape[2]
    packed = jnp.concatenate(
        [qkv_weight[0, 0], qkv_weight[0, 1], qkv_weight[0, 2], proj_weight[0].T,
         jnp.stack([attn_gain[0], attn_bias[0], moe_gain[0], moe_bias[0]], axis=1),
         router_weight[0], jnp.zeros((shard, 128 - 4 - experts), BF)],
        axis=1,
    )
    packed = gather_dp(packed)
    inner = gather_dp(inner_weight)[0]
    outert = gather_dp(outer_weight.transpose(0, 1, 3, 2))[0]
    qkv = jnp.stack([packed[:, j * wide:(j + 1) * wide] for j in range(3)])
    projt = packed[:, 3 * wide:4 * wide]
    smalls = packed[:, 4 * wide:]
    gain1, bias1, gain2, bias2 = (smalls[:, j].astype(F32) for j in range(4))
    router = smalls[:, 4:4 + experts]
    weights = (gain1, bias1, gain2, bias2, qkv, projt, router, inner, outert)

    def pad_rows(values, fill=0):
        return jnp.pad(
            values, ((0, 0), (0, ROWS - piece), (0, 0)), constant_values=fill
        )

    def local_order(table, fill):
        halves = table[0].reshape(images, 2, piece, 2)
        halves = jnp.where(side == 0, halves, halves[:, ::-1])
        halves = jnp.pad(
            halves, ((0, 0), (0, 0), (0, ROWS - piece), (0, 0)), constant_values=fill
        )
        return halves.reshape(images, 2 * ROWS, 2).transpose(0, 2, 1)

    routes = local_order(expert_ids, 0)
    slots = local_order(slot_ids, CAP)
    kept = slots < CAP
    codes = jnp.where(kept, routes * CAP + slots, -1)
    onehot = (codes[..., None] == jnp.arange(experts * CAP, dtype=jnp.int32)).astype(BF)
    hot = routes[..., None] == jnp.arange(experts, dtype=jnp.int32)
    index = jnp.arange(2 * ROWS, dtype=jnp.int32)
    half = jnp.where(side == 0, index // ROWS, 1 - index // ROWS)
    row = index % ROWS
    key_live = (row < piece) & (half * piece + row < LIVE)
    tables = (onehot, kept, hot, key_live)

    start = pad_rows(images_in.reshape(images, piece, features))
    last = pad_rows(out_grad.reshape(images, piece, features))
    early, _ = forward(start, weights, tables)
    received = lax.ppermute(early, "pipe", [(0, 1)])
    y, saved = forward(jnp.where(is_first, start, received), weights, tables)
    late = backward(last, saved, weights, tables)[0]
    received = lax.ppermute(late.astype(BF), "pipe", [(1, 0)])
    dz, grad_qkv, grad_projt, small, grad_inner, grad_outert = backward(
        jnp.where(is_first, received, last), saved, weights, tables
    )
    outer_out = scatter_dp(grad_outert[None])
    inner_out = scatter_dp(grad_inner[None])
    packed_grads = jnp.concatenate(
        [*grad_qkv, grad_projt, small.astype(BF),
         jnp.zeros((features, 128 - small.shape[1]), BF)],
        axis=1,
    )
    packed_out = scatter_dp(packed_grads).astype(F32)
    own_small = packed_out[:, 4 * wide:4 * wide + small.shape[1]]
    own_small = own_small + swap(own_small)

    def shape_out(values):
        return values[:, :piece].reshape(1, micro, local, piece, features)

    return (
        shape_out(y),
        shape_out(dz),
        own_small[:, 0][None],
        own_small[:, 1][None],
        jnp.stack([packed_out[:, j * wide:(j + 1) * wide] for j in range(3)])[None],
        packed_out[:, 3 * wide:4 * wide].T[None],
        own_small[:, 2][None],
        own_small[:, 3][None],
        own_small[:, 4:][None],
        inner_out.astype(F32),
        outer_out.astype(F32).transpose(0, 1, 3, 2),
    )


def solution(mesh):
    in_specs = (
        P(None, "dp", "tensor", None),
        P(None, "dp", "tensor", None),
        P("pipe", "dp"),
        P("pipe", "dp"),
        P("pipe", None, "dp", "tensor"),
        P("pipe", "tensor", "dp"),
        P("pipe", "dp"),
        P("pipe", "dp"),
        P("pipe", "dp", None),
        P("pipe", None, "dp", "tensor"),
        P("pipe", None, "tensor", "dp"),
        P("pipe", None, "dp", None, None),
        P("pipe", None, "dp", None, None),
    )
    out_specs = (
        P("pipe", None, "dp", "tensor", None),
        P("pipe", None, "dp", "tensor", None),
        P("pipe", "dp"),
        P("pipe", "dp"),
        P("pipe", None, "dp", "tensor"),
        P("pipe", "tensor", "dp"),
        P("pipe", "dp"),
        P("pipe", "dp"),
        P("pipe", "dp", None),
        P("pipe", None, "dp", "tensor"),
        P("pipe", None, "tensor", "dp"),
    )
    return jax.shard_map(body, mesh=mesh, in_specs=in_specs, out_specs=out_specs, check_vma=False)
```

time: 1800 us -> 991 us (0.55)
  waiting for transfers between devices: 1090 us -> 712 us
  blocking collectives: 142 us -> 0 us
  other arithmetic: 139 us -> 25.2 us
  local copies, waits for them, and re-layouts: 180 us -> 74.5 us
  matrix products: 186 us -> 144 us
    unnamed x38 -> x7, waiting for transfers between devices: 681 us -> 43.2 us
    reduce_scatter x1 -> x2, waiting for transfers between devices: 162 us -> 325 us  [scatter_dp(): lax.psum_scatter(full, 'dp', scatter_dimension=full.ndim - 2, tiled=True)]
    all_gather x14 -> x0, blocking collectives: 93.2 us -> none  [the longest x1 32.5 us: body(): lax.all_gather(proj_weight, 'dp', axis=2, tiled=True)]
    all_gather x3, waiting for transfers between devices: 235 us -> 305 us  [gather_dp(): return lax.all_gather(shard, 'dp', axis=shard.ndim - 2, tiled=True)]
    reduce_sum x49 -> x18, other arithmetic: 70.5 us -> 8.95 us  [the longest x4 3.1 us: norm_stats(): centre = values - jnp.mean(values, axis=-1, keepdims=True)]
    dot_general x69 -> x45, matrix products: 186 us -> 134 us  [the longest x42 132 us: dot(): return jnp.einsum(spec, left, right, preferred_element_type=F32)]
    unnamed x7 -> x0, blocking collectives: 45.7 us -> none
    unnamed x517 -> x146, local copies, waits for them, and re-layouts: 54.9 us -> 25.2 us
  transfers between devices with their start and end apart: 28 -> 25, of which waited for: 18 -> 21; matrix products, arithmetic and copies ran while one was open for 14% -> 6% of each run, Pallas kernels for 0% -> 0%
where the time goes in v1:
time: 991 us; the launch traced here: 980 us
  waiting for transfers between devices  712 us (72%)
  matrix products  144 us (15%)
  local copies, waits for them, and re-layouts  74.5 us (8%)
  other arithmetic  25.2 us (3%)
  between operations  15.8 us (2%)
    reduce_scatter x2, waiting for transfers between devices, scatter_dp(): lax.psum_scatter(full, 'dp', scatter_dimension=full.ndim - 2, tiled=True)  325 us
    all_gather x3, waiting for transfers between devices, gather_dp(): return lax.all_gather(shard, 'dp', axis=shard.ndim - 2, tiled=True)  305 us
    dot_general x42, matrix products, dot(): return jnp.einsum(spec, left, right, preferred_element_type=F32)  132 us
    unnamed x7, waiting for transfers between devices  43.2 us
    unnamed x146, local copies, waits for them, and re-layouts  25.2 us
  transfers between devices with their start and end apart: 25, of which 21 were waited for; matrix products, arithmetic and copies ran while one was open for 6% of the time, Pallas kernels for 0%

profile of v1, /device:TPU:0, one launch (start us, length us, event | category | flops | bytes accessed | tf_op | source)
XLA Modules:
  0.0 980.0 jit_solution(14358156953575047224)
XLA Ops:
  15.9 54.8 %all-gather.4.cloned.1.call-done = bf16[768,1664]{1,0:T(8,128)(2,1)} async-done(((bf16[96,1664]{1,0:T(8,128)(2,1)}), bf16[768,1664]{1,0:T(8,128)(2,1)}) %all-gather.4.cloned.1.call-update) | async-done | bytes 2555920 | tf_op jit(solution)/shard_map/all_gather | solution.py:155
  79.1 3.9 fusion.184
  98.3 111.3 %all-gather.8.cloned.1.call-done = bf16[1,4,768,1536]{3,2,1,0:T(8,128)(2,1)} async-done(((bf16[1,4,96,1536]{3,2,1,0:T(8,128)(2,1)}), bf16[1,4,768,1536]{3,2,1,0:T(8,128)(2,1)}) %all-gather.8.cloned.1.call-update) | async-done | bytes 9437200 | tf_op jit(solution)/shard_map/all_gather | solution.py:155
  209.6 138.5 %all-gather.6.cloned.1.call-done = bf16[1,4,768,1536]{3,2,1,0:T(8,128)(2,1)} async-done(((bf16[1,4,96,1536]{3,2,1,0:T(8,128)(2,1)}), bf16[1,4,768,1536]{3,2,1,0:T(8,128)(2,1)}) %all-gather.6.cloned.1.call-update) | async-done | bytes 9437200 | tf_op jit(solution)/shard_map/all_gather | solution.py:155
  348.1 13.1 %fusion.55 = bf16[4,256,768]{2,1,0:T(8,128)(2,1)} fusion(bf16[1,4,768,1536]{3,2,1,0:T(8,128)(2,1)} %all-gather.8.cloned.1.call-done, bf16[4,256,768]{2,1,0:T(8,128)(2,1)} %bitcast.357, bf16[1,4,768,1536]{3,2,1,0:T(8,128)(2,1)} %all-gather.6.cloned.1.call-done), kind=kOutput, calls=%fused_computation.69 | convolution fusion | flops 4846780416 | bytes 22020096 | tf_op jit(solution)/shard_map/ecf,edf->ecd/dot_general | solution.py:16
  367.7 3.4 collective-permute-start.4
  371.1 8.9 collective-permute-done.4
  384.0 2.7 fusion.77
  387.5 2.9 fusion.186
  400.2 4.9 copy.287
  405.1 3.7 reshape.287
  408.9 9.4 fusion.16
  418.3 8.4 fusion.60
  428.2 2.8 fusion.39
  432.6 2.7 bitcast_convert_fusion.1
  436.6 22.2 %fusion.47 = bf16[4,256,768]{2,1,0:T(8,128)(2,1)} fusion(bf16[1,4,768,1536]{3,2,1,0:T(8,128)(2,1)} %all-gather.6.cloned.1.call-done, bf16[4,256,768]{2,1,0:T(8,128)(2,1)} %bitcast.362, bf16[1,4,768,1536]{3,2,1,0:T(8,128)(2,1)} %all-gather.8.cloned.1.call-done, f32[4,256,1536]{2,1,0:T(8,128)} %fusion.16), kind=kOutput, calls=%fused_computation.67 | convolution fusion | flops 4862509056 | bytes 28311552 | tf_op jit(solution)/shard_map/ecf,edf->ecd/dot_general | solution.py:16
  469.7 2.9 multiply_reduce_fusion.1
  482.4 11.9 %collective-permute-done.13 = bf16[2,128,768]{2,1,0:T(8,128)(2,1)S(1)} collective-permute-done((bf16[2,128,768]{2,1,0:T(8,128)(2,1)S(1)}, bf16[2,128,768]{2,1,0:T(8,128)(2,1)S(1)}, u32[]{:S(2)}, u32[]{:S(2)}) %collective-permute-start.13) | collective-permute-done | bytes 393248 | tf_op jit(solution)/shard_map/ppermute | solution.py:230
  500.3 5.0 copy.308
  505.3 3.8 reshape.301
  509.1 10.0 %multiply_convert_fusion = bf16[4,256,1536]{2,1,0:T(8,128)(2,1)S(1)} fusion(bf16[4,256,768]{1,2,0:T(8,128)(2,1)} %reshape.301, bf16[1,4,768,1536]{3,2,1,0:T(8,128)(2,1)} %all-gather.8.cloned.1.call-done, f32[4,256,1536]{2,1,0:T(8,128)} %fusion.16), kind=kOutput, calls=%fused_computation.36 | convolution fusion | flops 2445803520 | bytes 20447232 | tf_op jit(solution)/shard_map/ecd,edf->ecf/dot_general | solution.py:16
  519.0 7.5 fusion.52
  538.7 2.9 multiply_reduce_fusion
  554.6 11.3 %concatenate.50 = bf16[768,1664]{0,1:T(8,128)(2,1)S(1)} concatenate(bf16[768,384]{0,1:T(8,128)(2,1)} %fusion.78, bf16[768,384]{0,1:T(8,128)(2,1)} %fusion.79, bf16[768,384]{0,1:T(8,128)(2,1)} %fusion.80, bf16[768,384]{0,1:T(8,128)(2,1)} %fusion.81, bf16[768,1]{0,1:T(2,128)(2,1)S(1)} %stack.44, bf16[768,1]{0,1:T(2,128)(2,1)S(1)} %stack.45, bf16[768,1]{0,1:T(2,128)(2,1)S(1)} %stack.46, ...), dimensions={1} | concatenate | bytes 5111808 | tf_op jit(solution)/shard_map/concatenate | solution.py:236
  565.9 4.2 copy.362
  571.5 7.2 convert_bitcast_fusion.1
  580.1 9.3 convert_bitcast_fusion
  596.1 41.7 %reduce-scatter.10.cloned.1.call-done = bf16[96,1664]{1,0:T(8,128)(2,1)} async-done(((bf16[768,1664]{1,0:T(8,128)(2,1)}), bf16[96,1664]{1,0:T(8,128)(2,1)}) %reduce-scatter.10.cloned.1.call-update) | async-done | bytes 319504
  642.2 161.5 %reduce-scatter.6.cloned.1.call-done = bf16[1,4,96,1536]{3,2,1,0:T(8,128)(2,1)} async-done(((bf16[1,4,768,1536]{3,2,1,0:T(8,128)(2,1)}), bf16[1,4,96,1536]{3,2,1,0:T(8,128)(2,1)}) %reduce-scatter.6.cloned.1.call-update) | async-done | bytes 1179664 | tf_op jit(solution)/shard_map/reduce_scatter | solution.py:159
  803.6 3.0 convert_element_type.349
  806.6 163.1 %reduce-scatter.8.cloned.1.call-done = bf16[1,4,96,1536]{3,2,1,0:T(8,128)(2,1)} async-done(((bf16[1,4,768,1536]{3,2,1,0:T(8,128)(2,1)}), bf16[1,4,96,1536]{3,2,1,0:T(8,128)(2,1)}) %reduce-scatter.8.cloned.1.call-update) | async-done | bytes 1179664 | tf_op jit(solution)/shard_map/reduce_scatter | solution.py:159
  969.7 3.0 convert_bitcast_fusion.2
  (333 shorter events, 122.2 us)
Async XLA Ops:
  7.2 8.3 copy-start.55
  7.2 63.5 %all-gather.4.cloned.1.call-start = ((), (), s32[]{:S(2)}) async-start(), calls=%async_computation.3 | async-start | bytes 2875392 | tf_op jit(solution)/shard_map/all_gather | solution.py:155
  13.9 195.7 %all-gather.8.cloned.1.call-start = ((), (), s32[]{:S(2)}) async-start(), calls=%async_computation.5 | async-start | bytes 10616832 | tf_op jit(solution)/shard_map/all_gather | solution.py:155
  14.7 333.4 %all-gather.6.cloned.1.call-start = ((), (), s32[]{:S(2)}) async-start(), calls=%async_computation.4 | async-start | bytes 10616832 | tf_op jit(solution)/shard_map/all_gather | solution.py:155
  15.4 622.4 %reduce-scatter.10.cloned.1.call-start = ((), (), s32[]{:S(2)}) async-start(), calls=%async_computation.8 | async-start | bytes 2875392
  15.5 58.9 %copy-start.15 = (bf16[2,1,100,768]{3,2,0,1:T(8,128)(2,1)}, bf16[2,1,100,768]{3,2,0,1:T(8,128)(2,1)S(1)}, u32[]{:S(2)}) copy-start(bf16[2,1,100,768]{3,2,0,1:T(8,128)(2,1)S(1)} %copy.381) | copy-start | bytes 921604
  72.7 3.4 collective-permute-start
  72.8 6.3 copy-start.65
  87.5 2.6 collective-permute-start.1
  92.2 1.8 collective-permute-start.2
  364.4 2.4 collective-permute-start.3
  367.7 12.3 %collective-permute-start.4 = (bf16[2,128,768]{2,1,0:T(8,128)(2,1)}, bf16[2,128,768]{2,1,0:T(8,128)(2,1)S(1)}, u32[]{:S(2)}, u32[]{:S(2)}) collective-permute-start(bf16[2,128,768]{2,1,0:T(8,128)(2,1)} %fusion.106), channel_id=1, source_target_pairs={{0,16},{1,17},{2,18},{3,19},{4,20},{5,21},{6,22},{7,23},{8,24},{9,... | collective-permute-start | bytes 1179656 | tf_op jit(solution)/shard_map/ppermute | solution.py:227
  382.2 4.5 copy-start.48
  382.2 5.3 copy-start.66
  382.2 1.8 collective-permute-start.5
  393.6 2.4 collective-permute-start.6
  394.1 2.7 collective-permute-start.9
  396.6 1.8 collective-permute-start.7
  462.1 1.8 collective-permute-start.10
  464.7 1.8 collective-permute-start.11
  478.0 1.8 collective-permute-start.12
  480.9 15.5 %copy-start.10 = (f32[2,2,256,768]{3,2,1,0:T(8,128)S(1)}, f32[2,2,256,768]{3,2,1,0:T(8,128)}, u32[]{:S(2)}) copy-start(f32[2,2,256,768]{3,2,1,0:T(8,128)} %get-tuple-element.131) | copy-start | bytes 9437188
  480.9 13.4 %collective-permute-start.13 = (bf16[2,128,768]{2,1,0:T(8,128)(2,1)S(1)}, bf16[2,128,768]{2,1,0:T(8,128)(2,1)S(1)}, u32[]{:S(2)}, u32[]{:S(2)}) collective-permute-start(bf16[2,128,768]{2,1,0:T(8,128)(2,1)S(1)} %add_convert_fusion), channel_id=1, source_target_pairs={{16,0},{17,1},{18,2},{19,3},{20,4},{21,5},{22,6},{23,7},{24,8},{25... | collective-permute-start | bytes 1179656 | tf_op jit(solution)/shard_map/ppermute | solution.py:230
  494.4 1.8 collective-permute-start.14
  519.0 7.6 copy-start.19
  529.4 1.8 collective-permute-start.15
  532.9 1.7 collective-permute-start.16
  546.9 5.7 collective-permute-start.17
  570.1 233.6 %reduce-scatter.6.cloned.1.call-start = ((), (), s32[]{:S(2)}) async-start(), calls=%async_computation.6 | async-start | bytes 10616832 | tf_op jit(solution)/shard_map/reduce_scatter | solution.py:159
  578.7 391.0 %reduce-scatter.8.cloned.1.call-start = ((), (), s32[]{:S(2)}) async-start(), calls=%async_computation.7 | async-start | bytes 10616832 | tf_op jit(solution)/shard_map/reduce_scatter | solution.py:159
  590.9 2.4 collective-permute-start.8
  639.1 2.0 collective-permute-start.18
  (60 other events, 130.2 us)
Sparse Core Ops, SparseCore 0:
  14.0 56.6 all-gather.3
  72.9 136.6 all-gather.7
  211.8 136.2 all-gather.5
  570.2 67.5 reduce-scatter.9
  641.2 162.3 reduce-scatter.5
  807.1 162.5 reduce-scatter.7

commit v2 on v1

--- a/solution.py
+++ b/solution.py
@@ -1,5 +1,6 @@
 import jax
 import jax.numpy as jnp
+import numpy as np
 from jax import lax
 from jax.sharding import PartitionSpec as P
 
@@ -7,6 +8,7 @@
 LIVE = 197
 CAP = 128
 ROWS = 128
+STREAMS = 2
 EPS = 1e-06
 BF = jnp.bfloat16
 F32 = jnp.float32
@@ -90,7 +92,7 @@
     return y.astype(BF), saved
 
 
-def backward(dy, saved, weights, tables):
+def backward(dy, saved, weights, tables, weight_grads):
     gain1, bias1, gain2, bias2, qkv, projt, router, inner, outert = weights
     onehot, kept, hot, key_live, = tables
     (unit1, inv1, a1, q, k, v, probs, attended, unit2, inv2, a2, router_probs, gate,
@@ -106,6 +108,8 @@
     dexp = dexp.reshape(images, experts, CAP, features).transpose(1, 0, 2, 3)
     dexp = dexp.reshape(experts, images * CAP, features)
     grad_outert = dot("ecd,ecf->edf", dexp, act).astype(BF)
+    if weight_grads:
+        grad_outert, dexp = lax.optimization_barrier((grad_outert, dexp))
     grad_act = dot("ecd,edf->ecf", dexp, outert)
     tanh = gelu_parts(pre)
     slope = 0.5 * (1.0 + tanh) + 0.5 * pre * (1.0 - tanh * tanh) * (
@@ -113,6 +117,8 @@
     )
     dpre = (grad_act * slope).astype(BF)
     grad_inner = dot("ecd,ecf->edf", rows_e, dpre).astype(BF)
+    if weight_grads:
+        grad_inner, dpre = lax.optimization_barrier((grad_inner, dpre))
     drows = dot("ecf,edf->ecd", dpre, inner).astype(BF)
     drows = drows.reshape(experts, images, CAP, features).transpose(1, 0, 2, 3)
     drows = drows.reshape(images, experts * CAP, features)
@@ -157,6 +163,52 @@
 
 def scatter_dp(full):
     return lax.psum_scatter(full, "dp", scatter_dimension=full.ndim - 2, tiled=True)
+
+
+def ring_plan(count, forward_way):
+    order = list(range(0, count, 2)) + list(range(count - 1 - count % 2, 0, -2))
+    if not forward_way:
+        order = order[::-1]
+    links = [(order[i], order[(i + 1) % count]) for i in range(count)]
+    behind = np.zeros((count, count), np.int32)
+    for place, device in enumerate(order):
+        for steps in range(count):
+            behind[device, steps] = order[(place - steps) % count]
+    row = jnp.asarray(behind)[lax.axis_index("dp")]
+    return links, [row[steps] for steps in range(count)]
+
+
+def ring_gather(shard, forward_way):
+    count = lax.axis_size("dp")
+    links, behind = ring_plan(count, forward_way)
+    experts, depth, wide = shard.shape
+    moving = shard[:, None]
+    whole = jnp.zeros((experts, count, depth, wide), shard.dtype)
+    whole = lax.dynamic_update_slice_in_dim(whole, moving, behind[0], 1)
+    for step in range(1, count):
+        moving = lax.ppermute(moving, "dp", links)
+        whole = lax.dynamic_update_slice_in_dim(whole, moving, behind[step], 1)
+    return whole.reshape(experts, count * depth, wide)
+
+
+def ring_scatter(full, forward_way, streams):
+    count = lax.axis_size("dp")
+    links, behind = ring_plan(count, forward_way)
+    experts, depth, wide = full.shape
+    blocks = full.reshape(experts, count, depth // count, wide)
+    part = experts // streams
+    done = []
+    for stream in range(streams):
+        mine = blocks[stream * part:(stream + 1) * part]
+        moving = lax.dynamic_index_in_dim(mine, behind[1 % count], 1, keepdims=False)
+        for step in range(2, count + 1):
+            came = lax.ppermute(moving, "dp", links).astype(F32)
+            own = lax.dynamic_index_in_dim(mine, behind[step % count], 1, keepdims=False)
+            moving = came + own.astype(F32)
+            if step < count:
+                moving = moving.astype(BF)
+        done.append(moving.astype(F32))
+    return jnp.concatenate(done, axis=0)
 
 
 def body(
@@ -187,8 +239,8 @@
         axis=1,
     )
     packed = gather_dp(packed)
-    inner = gather_dp(inner_weight)[0]
-    outert = gather_dp(outer_weight.transpose(0, 1, 3, 2))[0]
+    inner = ring_gather(inner_weight[0], True)
+    outert = ring_gather(outer_weight[0].transpose(0, 2, 1), False)
     qkv = jnp.stack([packed[:, j * wide:(j + 1) * wide] for j in range(3)])
     projt = packed[:, 3 * wide:4 * wide]
     smalls = packed[:, 4 * wide:]
@@ -226,13 +278,13 @@
     early, _ = forward(start, weights, tables)
     received = lax.ppermute(early, "pipe", [(0, 1)])
     y, saved = forward(jnp.where(is_first, start, received), weights, tables)
-    late = backward(last, saved, weights, tables)[0]
+    late = backward(last, saved, weights, tables, False)[0]
     received = lax.ppermute(late.astype(BF), "pipe", [(1, 0)])
     dz, grad_qkv, grad_projt, small, grad_inner, grad_outert = backward(
-        jnp.where(is_first, received, last), saved, weights, tables
-    )
-    outer_out = scatter_dp(grad_outert[None])
-    inner_out = scatter_dp(grad_inner[None])
+        jnp.where(is_first, received, last), saved, weights, tables, True
+    )
+    outer_out = ring_scatter(grad_outert, False, STREAMS)
+    inner_out = ring_scatter(grad_inner, True, STREAMS)
     packed_grads = jnp.concatenate(
         [*grad_qkv, grad_projt, small.astype(BF),
          jnp.zeros((features, 128 - small.shape[1]), BF)],
@@ -255,8 +307,8 @@
         own_small[:, 2][None],
         own_small[:, 3][None],
         own_small[:, 4:][None],
-        inner_out.astype(F32),
-        outer_out.astype(F32).transpose(0, 1, 3, 2),
+        inner_out[None],
+        outer_out.transpose(0, 2, 1)[None],
     )
 
 

time: 991 us -> 675 us (0.68)
  waiting for transfers between devices: 712 us -> 234 us
  local copies, waits for them, and re-layouts: 74.5 us -> 131 us
  starting transfers between devices: 8.55 us -> 58.9 us
  other arithmetic: 25.2 us -> 64.1 us
  between operations: 15.8 us -> 46.4 us
  matrix products: 144 us -> 128 us
    reduce_scatter x2 -> x0, waiting for transfers between devices: 325 us -> none  [scatter_dp(): lax.psum_scatter(full, 'dp', scatter_dimension=full.ndim - 2, tiled=True)]
    all_gather x3 -> x1, waiting for transfers between devices: 305 us -> 0.01 us  [gather_dp(): return lax.all_gather(shard, 'dp', axis=shard.ndim - 2, tiled=True)]
    ppermute x0 -> x42, waiting for transfers between devices: none -> 201 us  [the longest x28 104 us: ring_scatter(): came = lax.ppermute(moving, 'dp', links).astype(F32)]
    ppermute x0 -> x42, starting transfers between devices: none -> 51.8 us  [the longest x28 36.3 us: ring_scatter(): came = lax.ppermute(moving, 'dp', links).astype(F32)]
    unnamed x7 -> x3, waiting for transfers between devices: 43.2 us -> 0.03 us
    convert_element_type x1 -> x24, other arithmetic: 2.96 us -> 35.7 us  [ring_scatter(): moving = moving.astype(BF)]
    dynamic_update_slice x0 -> x16, local copies, waits for them, and re-layouts: none -> 31.8 us  [the longest x14 29.7 us: ring_gather(): whole = lax.dynamic_update_slice_in_dim(whole, moving, behind[step], 1)]
    dot_general x42, matrix products: 132 us -> 113 us  [dot(): return jnp.einsum(spec, left, right, preferred_element_type=F32)]
  transfers between devices with their start and end apart: 25 -> 63, of which waited for: 21 -> 32; matrix products, arithmetic and copies ran while one was open for 6% -> 31% of each run, Pallas kernels for 0% -> 0%
where the time goes in v2:
time: 675 us; the launch traced here: 663 us
  waiting for transfers between devices  234 us (35%)
  local copies, waits for them, and re-layouts  131 us (19%)
  matrix products  128 us (19%)
  other arithmetic  64.1 us (9%)
  starting transfers between devices  58.9 us (9%)
  between operations  46.4 us (7%)
    dot_general x42, matrix products, dot(): return jnp.einsum(spec, left, right, preferred_element_type=F32)  113 us
    ppermute x28, waiting for transfers between devices, ring_scatter(): came = lax.ppermute(moving, 'dp', links).astype(F32)  104 us
    ppermute x14, waiting for transfers between devices, ring_gather(): moving = lax.ppermute(moving, 'dp', links)  97.5 us
    ppermute x28, starting transfers between devices, ring_scatter(): came = lax.ppermute(moving, 'dp', links).astype(F32)  36.3 us
    convert_element_type x24, other arithmetic, ring_scatter(): moving = moving.astype(BF)  35.7 us
    dynamic_update_slice x14, local copies, waits for them, and re-layouts, ring_gather(): whole = lax.dynamic_update_slice_in_dim(whole, moving, behind[step], 1)  29.7 us
    unnamed x130, local copies, waits for them, and re-layouts  25.8 us
    ppermute x14, starting transfers between devices, ring_gather(): moving = lax.ppermute(moving, 'dp', links)  15.5 us
  transfers between devices with their start and end apart: 63, of which 32 were waited for; matrix products, arithmetic and copies ran while one was open for 31% of the time, Pallas kernels for 0%

profile of v2, /device:TPU:0, one launch (start us, length us, event | category | flops | bytes accessed | tf_op | source)
XLA Modules:
  0.0 662.5 jit_solution(17161979958977512667)
XLA Ops:
  24.8 4.7 broadcast.206.clone
  30.5 23.0 %collective-permute-done.10 = bf16[4,1,96,1536]{3,2,0,1:T(8,128)(2,1)} collective-permute-done((bf16[4,1,96,1536]{3,2,0,1:T(8,128)(2,1)}, bf16[4,1,96,1536]{3,2,0,1:T(8,128)(2,1)}, u32[]{:S(2)}, u32[]{:S(2)}) %collective-permute-start.10) | collective-permute-done | bytes 1179680 | tf_op jit(solution)/shard_map/ppermute | solution.py:189
  84.8 4.8 broadcast.206.clone.1
  93.0 8.6 %collective-permute-done.11 = bf16[4,1,96,1536]{3,2,0,1:T(8,128)(2,1)} collective-permute-done((bf16[4,1,96,1536]{3,2,0,1:T(8,128)(2,1)}, bf16[4,1,96,1536]{3,2,0,1:T(8,128)(2,1)}, u32[]{:S(2)}, u32[]{:S(2)}) %collective-permute-start.11) | collective-permute-done | bytes 1179680 | tf_op jit(solution)/shard_map/ppermute | solution.py:189
  109.5 19.8 %collective-permute-done.12 = bf16[4,1,96,1536]{3,2,0,1:T(8,128)(2,1)} collective-permute-done((bf16[4,1,96,1536]{3,2,0,1:T(8,128)(2,1)}, bf16[4,1,96,1536]{3,2,0,1:T(8,128)(2,1)}, u32[]{:S(2)}, u32[]{:S(2)}) %collective-permute-start.12) | collective-permute-done | bytes 1179680 | tf_op jit(solution)/shard_map/ppermute | solution.py:189
  147.5 8.5 %collective-permute-done.13 = bf16[4,1,96,1536]{3,2,0,1:T(8,128)(2,1)} collective-permute-done((bf16[4,1,96,1536]{3,2,0,1:T(8,128)(2,1)}, bf16[4,1,96,1536]{3,2,0,1:T(8,128)(2,1)}, u32[]{:S(2)}, u32[]{:S(2)}) %collective-permute-start.13) | collective-permute-done | bytes 1179680 | tf_op jit(solution)/shard_map/ppermute | solution.py:189
  176.2 5.9 collective-permute-done.14
  192.2 15.4 %collective-permute-done.15 = bf16[4,1,96,1536]{3,2,0,1:T(8,128)(2,1)} collective-permute-done((bf16[4,1,96,1536]{3,2,0,1:T(8,128)(2,1)}, bf16[4,1,96,1536]{3,2,0,1:T(8,128)(2,1)}, u32[]{:S(2)}, u32[]{:S(2)}) %collective-permute-start.15) | collective-permute-done | bytes 1179680 | tf_op jit(solution)/shard_map/ppermute | solution.py:189
  216.0 16.2 %collective-permute-done.16 = bf16[4,1,96,1536]{3,2,0,1:T(8,128)(2,1)S(1)} collective-permute-done((bf16[4,1,96,1536]{3,2,0,1:T(8,128)(2,1)}, bf16[4,1,96,1536]{3,2,0,1:T(8,128)(2,1)S(1)}, u32[]{:S(2)}, u32[]{:S(2)}) %collective-permute-start.16) | collective-permute-done | bytes 1179680 | tf_op jit(solution)/shard_map/ppermute | solution.py:189
  234.6 13.1 %fusion.25 = bf16[4,256,768]{2,1,0:T(8,128)(2,1)} fusion(bf16[4,768,1536]{2,1,0:T(8,128)(2,1)} %bitcast.69, bf16[4,256,768]{2,1,0:T(8,128)(2,1)} %bitcast.569, bf16[4,768,1536]{2,1,0:T(8,128)(2,1)} %bitcast.47), kind=kOutput, calls=%fused_computation.53 | convolution fusion | flops 4846780416 | bytes 22020096 | tf_op jit(solution)/shard_map/ecf,edf->ecd/dot_general | solution.py:18
  256.8 8.9 %collective-permute-done.18 = bf16[2,128,768]{2,1,0:T(8,128)(2,1)S(1)} collective-permute-done((bf16[2,128,768]{2,1,0:T(8,128)(2,1)}, bf16[2,128,768]{2,1,0:T(8,128)(2,1)S(1)}, u32[]{:S(2)}, u32[]{:S(2)}) %collective-permute-start.18) | collective-permute-done | bytes 393248 | tf_op jit(solution)/shard_map/ppermute | solution.py:279
  286.7 5.1 copy.483
  295.5 9.5 %fusion.183 = f32[4,256,1536]{2,1,0:T(8,128)} fusion(bf16[4,256,768]{1,2,0:T(8,128)(2,1)} %reshape.421, bf16[4,768,1536]{2,1,0:T(8,128)(2,1)} %bitcast.47), kind=kOutput, calls=%fused_computation.390 | convolution fusion | flops 2415919104 | bytes 17301504 | tf_op jit(solution)/shard_map/ecd,edf->ecf/dot_general | solution.py:18
  305.0 8.4 %convolution_convert_fusion.4 = bf16[4,256,768]{2,1,0:T(8,128)(2,1)S(1)} fusion(bf16[4,768,1536]{2,1,0:T(8,128)(2,1)} %bitcast.69, f32[4,256,1536]{2,1,0:T(8,128)} %fusion.183), kind=kOutput, calls=%fused_computation.56 | convolution fusion | flops 2430861312 | bytes 17301504 | tf_op jit(solution)/shard_map/ecf,edf->ecd/dot_general | solution.py:18
  323.3 13.1 %convolution_convert_fusion.3 = bf16[4,256,768]{2,1,0:T(8,128)(2,1)} fusion(bf16[4,768,1536]{2,1,0:T(8,128)(2,1)} %bitcast.47, bf16[4,256,768]{2,1,0:T(8,128)(2,1)} %bitcast.577, bf16[4,768,1536]{2,1,0:T(8,128)(2,1)} %bitcast.69, f32[4,256,1536]{2,1,0:T(8,128)} %fusion.183), kind=kOutput, calls=%fused_computation.55 | convolution fusion | flops 4862509056 | bytes 28311552 | tf_op jit(solution)/shard_map/ecf,edf->ecd/dot_general | solution.py:18
  360.1 11.9 %collective-permute-done.27 = bf16[2,128,768]{2,1,0:T(8,128)(2,1)S(1)} collective-permute-done((bf16[2,128,768]{2,1,0:T(8,128)(2,1)S(1)}, bf16[2,128,768]{2,1,0:T(8,128)(2,1)S(1)}, u32[]{:S(2)}, u32[]{:S(2)}) %collective-permute-start.27) | collective-permute-done | bytes 393248 | tf_op jit(solution)/shard_map/ppermute | solution.py:282
  377.6 5.6 convolution_convert_fusion.1
  383.2 7.3 %multiply_convert_fusion = bf16[4,256,1536]{2,1,0:T(8,128)(2,1)S(1)} fusion(bf16[4,256,768]{2,1,0:T(8,128)(2,1)S(1)} %bitcast.571, bf16[4,768,1536]{2,1,0:T(8,128)(2,1)} %bitcast.69, f32[4,256,1536]{2,1,0:T(8,128)S(1)} %bitcast.551), kind=kOutput, calls=%fused_computation.20 | convolution fusion | flops 2445803520 | bytes 20447232 | tf_op jit(solution)/shard_map/ecd,edf->ecf/dot_general | solution.py:18
  390.5 5.1 convolution_convert_fusion
  395.6 6.4 convolution_convert_fusion.2
  405.8 6.6 fusion.170
  419.6 6.5 fusion.169
  436.0 8.3 %collective-permute-done.40 = bf16[2,96,1536]{2,1,0:T(8,128)(2,1)} collective-permute-done((bf16[2,96,1536]{2,1,0:T(8,128)(2,1)}, bf16[2,96,1536]{2,1,0:T(8,128)(2,1)}, u32[]{:S(2)}, u32[]{:S(2)}) %collective-permute-start.40) | collective-permute-done | bytes 589856 | tf_op jit(solution)/shard_map/ppermute | solution.py:205
  491.4 11.3 %concatenate.56 = bf16[768,1664]{0,1:T(8,128)(2,1)S(1)} concatenate(bf16[768,384]{0,1:T(8,128)(2,1)} %fusion.43, bf16[768,384]{0,1:T(8,128)(2,1)} %fusion.44, bf16[768,384]{0,1:T(8,128)(2,1)} %fusion.45, bf16[768,384]{0,1:T(8,128)(2,1)} %fusion.46, bf16[768,1]{0,1:T(2,128)(2,1)S(1)} %stack.44, bf16[768,1]{0,1:T(2,128)(2,1)S(1)} %stack.45, bf16[768,1]{0,1:T(2,128)(2,1)S(1)} %stack.46, ...), dimensions={1} | concatenate | bytes 5111808 | tf_op jit(solution)/shard_map/concatenate | solution.py:288
  516.8 16.5 %collective-permute-done.36 = bf16[2,96,1536]{2,1,0:T(8,128)(2,1)S(1)} collective-permute-done((bf16[2,96,1536]{2,1,0:T(8,128)(2,1)S(1)}, bf16[2,96,1536]{2,1,0:T(8,128)(2,1)S(1)}, u32[]{:S(2)}, u32[]{:S(2)}) %collective-permute-start.36) | collective-permute-done | bytes 589856 | tf_op jit(solution)/shard_map/ppermute | solution.py:205
  537.5 19.8 %collective-permute-done.43 = bf16[2,96,1536]{2,1,0:T(8,128)(2,1)S(1)} collective-permute-done((bf16[2,96,1536]{2,1,0:T(8,128)(2,1)S(1)}, bf16[2,96,1536]{2,1,0:T(8,128)(2,1)S(1)}, u32[]{:S(2)}, u32[]{:S(2)}) %collective-permute-start.43) | collective-permute-done | bytes 589856 | tf_op jit(solution)/shard_map/ppermute | solution.py:205
  573.7 8.9 %collective-permute-done.44 = bf16[2,96,1536]{2,1,0:T(8,128)(2,1)S(1)} collective-permute-done((bf16[2,96,1536]{2,1,0:T(8,128)(2,1)S(1)}, bf16[2,96,1536]{2,1,0:T(8,128)(2,1)S(1)}, u32[]{:S(2)}, u32[]{:S(2)}) %collective-permute-start.44) | collective-permute-done | bytes 589856 | tf_op jit(solution)/shard_map/ppermute | solution.py:205
  587.6 6.9 %collective-permute-done.58 = bf16[2,96,1536]{2,1,0:T(8,128)(2,1)S(1)} collective-permute-done((bf16[2,96,1536]{2,1,0:T(8,128)(2,1)S(1)}, bf16[2,96,1536]{2,1,0:T(8,128)(2,1)S(1)}, u32[]{:S(2)}, u32[]{:S(2)}) %collective-permute-start.58) | collective-permute-done | bytes 589856 | tf_op jit(solution)/shard_map/ppermute | solution.py:205
  596.2 9.5 %collective-permute-done.38 = bf16[2,96,1536]{2,1,0:T(8,128)(2,1)S(1)} collective-permute-done((bf16[2,96,1536]{2,1,0:T(8,128)(2,1)S(1)}, bf16[2,96,1536]{2,1,0:T(8,128)(2,1)S(1)}, u32[]{:S(2)}, u32[]{:S(2)}) %collective-permute-start.38) | collective-permute-done | bytes 589856 | tf_op jit(solution)/shard_map/ppermute | solution.py:205
  609.4 8.9 %collective-permute-done.45 = bf16[2,96,1536]{2,1,0:T(8,128)(2,1)S(1)} collective-permute-done((bf16[2,96,1536]{2,1,0:T(8,128)(2,1)S(1)}, bf16[2,96,1536]{2,1,0:T(8,128)(2,1)S(1)}, u32[]{:S(2)}, u32[]{:S(2)}) %collective-permute-start.45) | collective-permute-done | bytes 589856 | tf_op jit(solution)/shard_map/ppermute | solution.py:205
  626.1 4.8 collective-permute-done.39
  632.2 9.4 %collective-permute-done.46 = bf16[2,96,1536]{2,1,0:T(8,128)(2,1)S(1)} collective-permute-done((bf16[2,96,1536]{2,1,0:T(8,128)(2,1)S(1)}, bf16[2,96,1536]{2,1,0:T(8,128)(2,1)S(1)}, u32[]{:S(2)}, u32[]{:S(2)}) %collective-permute-start.46) | collective-permute-done | bytes 589856 | tf_op jit(solution)/shard_map/ppermute | solution.py:205
  (444 shorter events, 297.4 us)
Async XLA Ops:
  7.2 126.5 %all-gather.2.cloned.1.call-start = ((), (), s32[]{:S(2)}) async-start(), calls=%async_computation.1 | async-start | bytes 2875392 | tf_op jit(solution)/shard_map/all_gather | solution.py:161
  13.9 637.0 %reduce-scatter.4.cloned.1.call-start = ((), (), s32[]{:S(2)}) async-start(), calls=%async_computation.2 | async-start | bytes 2875392
  13.9 39.6 %collective-permute-start.10 = (bf16[4,1,96,1536]{3,2,0,1:T(8,128)(2,1)}, bf16[4,1,96,1536]{3,2,0,1:T(8,128)(2,1)}, u32[]{:S(2)}, u32[]{:S(2)}) collective-permute-start(bf16[4,1,96,1536]{3,2,0,1:T(8,128)(2,1)} %bitcast.580), channel_id=1, source_target_pairs={{1,3},{3,5},{5,7},{7,6},{6,4},{4,2},{2,0},{0,1},{9,11},{11,13},{13... | collective-permute-start | bytes 3538952 | tf_op jit(solution)/shard_map/ppermute | solution.py:189
  16.9 37.4 %collective-permute-start.3 = (bf16[4,1,96,1536]{3,2,0,1:T(8,128)(2,1)}, bf16[4,1,96,1536]{3,2,0,1:T(8,128)(2,1)}, u32[]{:S(2)}, u32[]{:S(2)}) collective-permute-start(bf16[4,1,96,1536]{3,2,0,1:T(8,128)(2,1)} %bitcast.581), channel_id=1, source_target_pairs={{0,2},{2,4},{4,6},{6,7},{7,5},{5,3},{3,1},{1,0},{8,10},{10,12},{12... | collective-permute-start | bytes 3538952 | tf_op jit(solution)/shard_map/ppermute | solution.py:189
  53.6 48.0 %collective-permute-start.11 = (bf16[4,1,96,1536]{3,2,0,1:T(8,128)(2,1)}, bf16[4,1,96,1536]{3,2,0,1:T(8,128)(2,1)}, u32[]{:S(2)}, u32[]{:S(2)}) collective-permute-start(bf16[4,1,96,1536]{3,2,0,1:T(8,128)(2,1)} %collective-permute-done.10), channel_id=1, source_target_pairs={{1,3},{3,5},{5,7},{7,6},{6,4},{4,2},{2,0},{0,1},{9,11},{11,13},{13... | collective-permute-start | bytes 3538952 | tf_op jit(solution)/shard_map/ppermute | solution.py:189
  54.3 47.3 %collective-permute-start.4 = (bf16[4,1,96,1536]{3,2,0,1:T(8,128)(2,1)}, bf16[4,1,96,1536]{3,2,0,1:T(8,128)(2,1)S(1)}, u32[]{:S(2)}, u32[]{:S(2)}) collective-permute-start(bf16[4,1,96,1536]{3,2,0,1:T(8,128)(2,1)} %collective-permute-done.3), channel_id=1, source_target_pairs={{0,2},{2,4},{4,6},{6,7},{7,5},{5,3},{3,1},{1,0},{8,10},{10,12},{12... | collective-permute-start | bytes 3538952 | tf_op jit(solution)/shard_map/ppermute | solution.py:189
  101.6 27.7 %collective-permute-start.12 = (bf16[4,1,96,1536]{3,2,0,1:T(8,128)(2,1)}, bf16[4,1,96,1536]{3,2,0,1:T(8,128)(2,1)}, u32[]{:S(2)}, u32[]{:S(2)}) collective-permute-start(bf16[4,1,96,1536]{3,2,0,1:T(8,128)(2,1)} %collective-permute-done.11), channel_id=1, source_target_pairs={{1,3},{3,5},{5,7},{7,6},{6,4},{4,2},{2,0},{0,1},{9,11},{11,13},{13... | collective-permute-start | bytes 3538952 | tf_op jit(solution)/shard_map/ppermute | solution.py:189
  101.6 27.9 %collective-permute-start.5 = (bf16[4,1,96,1536]{3,2,0,1:T(8,128)(2,1)S(1)}, bf16[4,1,96,1536]{3,2,0,1:T(8,128)(2,1)}, u32[]{:S(2)}, u32[]{:S(2)}) collective-permute-start(bf16[4,1,96,1536]{3,2,0,1:T(8,128)(2,1)S(1)} %collective-permute-done.4), channel_id=1, source_target_pairs={{0,2},{2,4},{4,6},{6,7},{7,5},{5,3},{3,1},{1,0},{8,10},{10,12},{12... | collective-permute-start | bytes 3538952 | tf_op jit(solution)/shard_map/ppermute | solution.py:189
  129.2 26.7 %collective-permute-start.13 = (bf16[4,1,96,1536]{3,2,0,1:T(8,128)(2,1)}, bf16[4,1,96,1536]{3,2,0,1:T(8,128)(2,1)}, u32[]{:S(2)}, u32[]{:S(2)}) collective-permute-start(bf16[4,1,96,1536]{3,2,0,1:T(8,128)(2,1)} %collective-permute-done.12), channel_id=1, source_target_pairs={{1,3},{3,5},{5,7},{7,6},{6,4},{4,2},{2,0},{0,1},{9,11},{11,13},{13... | collective-permute-start | bytes 3538952 | tf_op jit(solution)/shard_map/ppermute | solution.py:189
  129.5 27.1 %collective-permute-start.6 = (bf16[4,1,96,1536]{3,2,0,1:T(8,128)(2,1)}, bf16[4,1,96,1536]{3,2,0,1:T(8,128)(2,1)}, u32[]{:S(2)}, u32[]{:S(2)}) collective-permute-start(bf16[4,1,96,1536]{3,2,0,1:T(8,128)(2,1)} %collective-permute-done.5), channel_id=1, source_target_pairs={{0,2},{2,4},{4,6},{6,7},{7,5},{5,3},{3,1},{1,0},{8,10},{10,12},{12... | collective-permute-start | bytes 3538952 | tf_op jit(solution)/shard_map/ppermute | solution.py:189
  156.0 26.1 %collective-permute-start.14 = (bf16[4,1,96,1536]{3,2,0,1:T(8,128)(2,1)}, bf16[4,1,96,1536]{3,2,0,1:T(8,128)(2,1)}, u32[]{:S(2)}, u32[]{:S(2)}) collective-permute-start(bf16[4,1,96,1536]{3,2,0,1:T(8,128)(2,1)} %collective-permute-done.13), channel_id=1, source_target_pairs={{1,3},{3,5},{5,7},{7,6},{6,4},{4,2},{2,0},{0,1},{9,11},{11,13},{13... | collective-permute-start | bytes 3538952 | tf_op jit(solution)/shard_map/ppermute | solution.py:189
  156.6 26.1 %collective-permute-start.7 = (bf16[4,1,96,1536]{3,2,0,1:T(8,128)(2,1)}, bf16[4,1,96,1536]{3,2,0,1:T(8,128)(2,1)}, u32[]{:S(2)}, u32[]{:S(2)}) collective-permute-start(bf16[4,1,96,1536]{3,2,0,1:T(8,128)(2,1)} %collective-permute-done.6), channel_id=1, source_target_pairs={{0,2},{2,4},{4,6},{6,7},{7,5},{5,3},{3,1},{1,0},{8,10},{10,12},{12... | collective-permute-start | bytes 3538952 | tf_op jit(solution)/shard_map/ppermute | solution.py:189
  182.7 27.4 %collective-permute-start.8 = (bf16[4,1,96,1536]{3,2,0,1:T(8,128)(2,1)}, bf16[4,1,96,1536]{3,2,0,1:T(8,128)(2,1)}, u32[]{:S(2)}, u32[]{:S(2)}) collective-permute-start(bf16[4,1,96,1536]{3,2,0,1:T(8,128)(2,1)} %collective-permute-done.7), channel_id=1, source_target_pairs={{0,2},{2,4},{4,6},{6,7},{7,5},{5,3},{3,1},{1,0},{8,10},{10,12},{12... | collective-permute-start | bytes 3538952 | tf_op jit(solution)/shard_map/ppermute | solution.py:189
  377.4 89.1 %collective-permute-start.22 = (f32[2,128,768]{2,1,0:T(8,128)}, f32[2,128,768]{2,1,0:T(8,128)}, u32[]{:S(2)}, u32[]{:S(2)}) collective-permute-start(f32[2,128,768]{2,1,0:T(8,128)} %get-tuple-element.115), channel_id=1, source_target_pairs={{0,8},{8,0},{1,9},{9,1},{2,10},{10,2},{3,11},{11,3},{4,12},{12,4},... | collective-permute-start | bytes 2359304 | tf_op jit(solution)/shard_map/ppermute | solution.py:22
  417.8 26.6 %collective-permute-start.40 = (bf16[2,96,1536]{2,1,0:T(8,128)(2,1)}, bf16[2,96,1536]{2,1,0:T(8,128)(2,1)}, u32[]{:S(2)}, u32[]{:S(2)}) collective-permute-start(bf16[2,96,1536]{2,1,0:T(8,128)(2,1)} %dynamic-slice_bitcast_fusion.2), channel_id=1, source_target_pairs={{0,2},{2,4},{4,6},{6,7},{7,5},{5,3},{3,1},{1,0},{8,10},{10,12},{12... | collective-permute-start | bytes 1769480 | tf_op jit(solution)/shard_map/ppermute | solution.py:205
  444.4 32.6 %collective-permute-start.34 = (bf16[2,96,1536]{2,1,0:T(8,128)(2,1)}, bf16[2,96,1536]{2,1,0:T(8,128)(2,1)}, u32[]{:S(2)}, u32[]{:S(2)}) collective-permute-start(bf16[2,96,1536]{2,1,0:T(8,128)(2,1)} %fusion.75), channel_id=1, source_target_pairs={{0,2},{2,4},{4,6},{6,7},{7,5},{5,3},{3,1},{1,0},{8,10},{10,12},{12... | collective-permute-start | bytes 1769480 | tf_op jit(solution)/shard_map/ppermute | solution.py:205
  448.5 31.6 %collective-permute-start.41 = (bf16[2,96,1536]{2,1,0:T(8,128)(2,1)}, bf16[2,96,1536]{2,1,0:T(8,128)(2,1)}, u32[]{:S(2)}, u32[]{:S(2)}) collective-permute-start(bf16[2,96,1536]{2,1,0:T(8,128)(2,1)} %fusion.69), channel_id=1, source_target_pairs={{0,2},{2,4},{4,6},{6,7},{7,5},{5,3},{3,1},{1,0},{8,10},{10,12},{12... | collective-permute-start | bytes 1769480 | tf_op jit(solution)/shard_map/ppermute | solution.py:205
  455.2 28.9 %collective-permute-start.48 = (bf16[2,96,1536]{2,1,0:T(8,128)(2,1)}, bf16[2,96,1536]{2,1,0:T(8,128)(2,1)}, u32[]{:S(2)}, u32[]{:S(2)}) collective-permute-start(bf16[2,96,1536]{2,1,0:T(8,128)(2,1)} %fusion.63), channel_id=1, source_target_pairs={{1,3},{3,5},{5,7},{7,6},{6,4},{4,2},{2,0},{0,1},{9,11},{11,13},{13... | collective-permute-start | bytes 1769480 | tf_op jit(solution)/shard_map/ppermute | solution.py:205
  456.4 30.2 %collective-permute-start.55 = (bf16[2,96,1536]{2,1,0:T(8,128)(2,1)}, bf16[2,96,1536]{2,1,0:T(8,128)(2,1)}, u32[]{:S(2)}, u32[]{:S(2)}) collective-permute-start(bf16[2,96,1536]{2,1,0:T(8,128)(2,1)} %fusion.57), channel_id=1, source_target_pairs={{1,3},{3,5},{5,7},{7,6},{6,4},{4,2},{2,0},{0,1},{9,11},{11,13},{13... | collective-permute-start | bytes 1769480 | tf_op jit(solution)/shard_map/ppermute | solution.py:205
  478.3 28.5 %collective-permute-start.35 = (bf16[2,96,1536]{2,1,0:T(8,128)(2,1)S(1)}, bf16[2,96,1536]{2,1,0:T(8,128)(2,1)}, u32[]{:S(2)}, u32[]{:S(2)}) collective-permute-start(bf16[2,96,1536]{2,1,0:T(8,128)(2,1)S(1)} %fusion.74), channel_id=1, source_target_pairs={{0,2},{2,4},{4,6},{6,7},{7,5},{5,3},{3,1},{1,0},{8,10},{10,12},{12... | collective-permute-start | bytes 1769480 | tf_op jit(solution)/shard_map/ppermute | solution.py:205
  482.4 27.6 %collective-permute-start.42 = (bf16[2,96,1536]{2,1,0:T(8,128)(2,1)}, bf16[2,96,1536]{2,1,0:T(8,128)(2,1)}, u32[]{:S(2)}, u32[]{:S(2)}) collective-permute-start(bf16[2,96,1536]{2,1,0:T(8,128)(2,1)} %fusion.68), channel_id=1, source_target_pairs={{0,2},{2,4},{4,6},{6,7},{7,5},{5,3},{3,1},{1,0},{8,10},{10,12},{12... | collective-permute-start | bytes 1769480 | tf_op jit(solution)/shard_map/ppermute | solution.py:205
  486.4 26.8 %collective-permute-start.49 = (bf16[2,96,1536]{2,1,0:T(8,128)(2,1)}, bf16[2,96,1536]{2,1,0:T(8,128)(2,1)}, u32[]{:S(2)}, u32[]{:S(2)}) collective-permute-start(bf16[2,96,1536]{2,1,0:T(8,128)(2,1)} %fusion.62), channel_id=1, source_target_pairs={{1,3},{3,5},{5,7},{7,6},{6,4},{4,2},{2,0},{0,1},{9,11},{11,13},{13... | collective-permute-start | bytes 1769480 | tf_op jit(solution)/shard_map/ppermute | solution.py:205
  488.9 26.0 %collective-permute-start.56 = (bf16[2,96,1536]{2,1,0:T(8,128)(2,1)}, bf16[2,96,1536]{2,1,0:T(8,128)(2,1)}, u32[]{:S(2)}, u32[]{:S(2)}) collective-permute-start(bf16[2,96,1536]{2,1,0:T(8,128)(2,1)} %fusion.56), channel_id=1, source_target_pairs={{1,3},{3,5},{5,7},{7,6},{6,4},{4,2},{2,0},{0,1},{9,11},{11,13},{13... | collective-permute-start | bytes 1769480 | tf_op jit(solution)/shard_map/ppermute | solution.py:205
  511.4 45.9 %collective-permute-start.43 = (bf16[2,96,1536]{2,1,0:T(8,128)(2,1)S(1)}, bf16[2,96,1536]{2,1,0:T(8,128)(2,1)S(1)}, u32[]{:S(2)}, u32[]{:S(2)}) collective-permute-start(bf16[2,96,1536]{2,1,0:T(8,128)(2,1)S(1)} %fusion.67), channel_id=1, source_target_pairs={{0,2},{2,4},{4,6},{6,7},{7,5},{5,3},{3,1},{1,0},{8,10},{10,12},{12... | collective-permute-start | bytes 1769480 | tf_op jit(solution)/shard_map/ppermute | solution.py:205
  514.7 46.4 %collective-permute-start.50 = (bf16[2,96,1536]{2,1,0:T(8,128)(2,1)S(1)}, bf16[2,96,1536]{2,1,0:T(8,128)(2,1)S(1)}, u32[]{:S(2)}, u32[]{:S(2)}) collective-permute-start(bf16[2,96,1536]{2,1,0:T(8,128)(2,1)S(1)} %fusion.61), channel_id=1, source_target_pairs={{1,3},{3,5},{5,7},{7,6},{6,4},{4,2},{2,0},{0,1},{9,11},{11,13},{13... | collective-permute-start | bytes 1769480 | tf_op jit(solution)/shard_map/ppermute | solution.py:205
  516.3 46.6 %collective-permute-start.57 = (bf16[2,96,1536]{2,1,0:T(8,128)(2,1)S(1)}, bf16[2,96,1536]{2,1,0:T(8,128)(2,1)S(1)}, u32[]{:S(2)}, u32[]{:S(2)}) collective-permute-start(bf16[2,96,1536]{2,1,0:T(8,128)(2,1)S(1)} %fusion.55), channel_id=1, source_target_pairs={{1,3},{3,5},{5,7},{7,6},{6,4},{4,2},{2,0},{0,1},{9,11},{11,13},{13... | collective-permute-start | bytes 1769480 | tf_op jit(solution)/shard_map/ppermute | solution.py:205
  534.5 35.4 %collective-permute-start.37 = (bf16[2,96,1536]{2,1,0:T(8,128)(2,1)S(1)}, bf16[2,96,1536]{2,1,0:T(8,128)(2,1)S(1)}, u32[]{:S(2)}, u32[]{:S(2)}) collective-permute-start(bf16[2,96,1536]{2,1,0:T(8,128)(2,1)S(1)} %fusion.72), channel_id=1, source_target_pairs={{0,2},{2,4},{4,6},{6,7},{7,5},{5,3},{3,1},{1,0},{8,10},{10,12},{12... | collective-permute-start | bytes 1769480 | tf_op jit(solution)/shard_map/ppermute | solution.py:205
  564.1 30.5 %collective-permute-start.58 = (bf16[2,96,1536]{2,1,0:T(8,128)(2,1)S(1)}, bf16[2,96,1536]{2,1,0:T(8,128)(2,1)S(1)}, u32[]{:S(2)}, u32[]{:S(2)}) collective-permute-start(bf16[2,96,1536]{2,1,0:T(8,128)(2,1)S(1)} %fusion.54), channel_id=1, source_target_pairs={{1,3},{3,5},{5,7},{7,6},{6,4},{4,2},{2,0},{0,1},{9,11},{11,13},{13... | collective-permute-start | bytes 1769480 | tf_op jit(solution)/shard_map/ppermute | solution.py:205
  571.1 34.5 %collective-permute-start.38 = (bf16[2,96,1536]{2,1,0:T(8,128)(2,1)S(1)}, bf16[2,96,1536]{2,1,0:T(8,128)(2,1)S(1)}, u32[]{:S(2)}, u32[]{:S(2)}) collective-permute-start(bf16[2,96,1536]{2,1,0:T(8,128)(2,1)S(1)} %fusion.71), channel_id=1, source_target_pairs={{0,2},{2,4},{4,6},{6,7},{7,5},{5,3},{3,1},{1,0},{8,10},{10,12},{12... | collective-permute-start | bytes 1769480 | tf_op jit(solution)/shard_map/ppermute | solution.py:205
  583.8 34.5 %collective-permute-start.45 = (bf16[2,96,1536]{2,1,0:T(8,128)(2,1)S(1)}, bf16[2,96,1536]{2,1,0:T(8,128)(2,1)S(1)}, u32[]{:S(2)}, u32[]{:S(2)}) collective-permute-start(bf16[2,96,1536]{2,1,0:T(8,128)(2,1)S(1)} %fusion.65), channel_id=1, source_target_pairs={{0,2},{2,4},{4,6},{6,7},{7,5},{5,3},{3,1},{1,0},{8,10},{10,12},{12... | collective-permute-start | bytes 1769480 | tf_op jit(solution)/shard_map/ppermute | solution.py:205
  587.5 34.5 %collective-permute-start.52 = (bf16[2,96,1536]{2,1,0:T(8,128)(2,1)S(1)}, bf16[2,96,1536]{2,1,0:T(8,128)(2,1)S(1)}, u32[]{:S(2)}, u32[]{:S(2)}) collective-permute-start(bf16[2,96,1536]{2,1,0:T(8,128)(2,1)S(1)} %fusion.59), channel_id=1, source_target_pairs={{1,3},{3,5},{5,7},{7,6},{6,4},{4,2},{2,0},{0,1},{9,11},{11,13},{13... | collective-permute-start | bytes 1769480 | tf_op jit(solution)/shard_map/ppermute | solution.py:205
  595.7 28.0 %collective-permute-start.59 = (bf16[2,96,1536]{2,1,0:T(8,128)(2,1)S(1)}, bf16[2,96,1536]{2,1,0:T(8,128)(2,1)S(1)}, u32[]{:S(2)}, u32[]{:S(2)}) collective-permute-start(bf16[2,96,1536]{2,1,0:T(8,128)(2,1)S(1)} %fusion.53), channel_id=1, source_target_pairs={{1,3},{3,5},{5,7},{7,6},{6,4},{4,2},{2,0},{0,1},{9,11},{11,13},{13... | collective-permute-start | bytes 1769480 | tf_op jit(solution)/shard_map/ppermute | solution.py:205
  (90 other events, 836.5 us)
Sparse Core Ops, SparseCore 0:
  14.0 83.4 all-gather.1
  506.9 98.0 reduce-scatter.3

commit v3 on v2

--- a/solution.py
+++ b/solution.py
@@ -145,7 +145,16 @@
     dq = (dot("ihqk,ikhd->iqhd", dscores, k) * scale).astype(BF)
     dk = (dot("ihqk,iqhd->ikhd", dscores, q) * scale).astype(BF)
     flat = tuple(part.reshape(images, length, heads * HEAD_DIM) for part in (dq, dk, dv))
-    grad_qkv = tuple(dot("isd,ise->de", a1, part).astype(BF) for part in flat)
+    rings = None
+    if weight_grads:
+        rings = (RingScatter(grad_outert, False, STREAMS), RingScatter(grad_inner, True, STREAMS))
+        for ring in rings:
+            ring.advance()
+            ring.advance()
+        flat, rings[0].moving, rings[1].moving = lax.optimization_barrier(
+            (flat, rings[0].moving, rings[1].moving)
+        )
+    grad_qkv = dot("isd,ise->de", a1, jnp.concatenate(flat, axis=2)).astype(BF)
     da1 = sum(dot("ise,de->isd", part, qkv[j]) for j, part in enumerate(flat))
     da1 = sum_halves(da1, BF)
     grad_gain1 = jnp.sum(da1 * unit1, axis=(0, 1))
@@ -154,7 +163,7 @@
     small = jnp.concatenate(
         [jnp.stack([grad_gain1, grad_bias1, grad_gain2, grad_bias2], axis=1), grad_router], axis=1
     )
-    return dz, grad_qkv, grad_projt, small, grad_inner, grad_outert
+    return dz, grad_qkv, grad_projt, small, rings
 
 
 def gather_dp(shard):
@@ -191,24 +200,34 @@
     return whole.reshape(experts, count * depth, wide)
 
 
-def ring_scatter(full, forward_way, streams):
-    count = lax.axis_size("dp")
-    links, behind = ring_plan(count, forward_way)
-    experts, depth, wide = full.shape
-    blocks = full.reshape(experts, count, depth // count, wide)
-    part = experts // streams
-    done = []
-    for stream in range(streams):
-        mine = blocks[stream * part:(stream + 1) * part]
-        moving = lax.dynamic_index_in_dim(mine, behind[1 % count], 1, keepdims=False)
-        for step in range(2, count + 1):
-            came = lax.ppermute(moving, "dp", links).astype(F32)
-            own = lax.dynamic_index_in_dim(mine, behind[step % count], 1, keepdims=False)
-            moving = came + own.astype(F32)
-            if step < count:
-                moving = moving.astype(BF)
-        done.append(moving.astype(F32))
-    return jnp.concatenate(done, axis=0)
+class RingScatter:
+    def __init__(self, full, forward_way, streams):
+        self.count = lax.axis_size("dp")
+        self.links, self.behind = ring_plan(self.count, forward_way)
+        experts, depth, wide = full.shape
+        blocks = full.reshape(experts, self.count, depth // self.count, wide)
+        part = experts // streams
+        self.mine = [blocks[i * part:(i + 1) * part] for i in range(streams)]
+        self.moving = [self.block(mine, 1) for mine in self.mine]
+        self.step = 2
+
+    def block(self, mine, step):
+        place = self.behind[step % self.count]
+        return lax.dynamic_index_in_dim(mine, place, 1, keepdims=False)
+
+    def advance(self):
+        sums = []
+        for mine, moving in zip(self.mine, self.moving):
+            came = lax.ppermute(moving, "dp", self.links).astype(F32)
+            total = came + self.block(mine, self.step).astype(F32)
+            sums.append(total.astype(BF) if self.step < self.count else total)
+        self.moving = sums
+        self.step += 1
+
+    def finish(self):
+        while self.step <= self.count:
+            self.advance()
+        return jnp.concatenate(self.moving, axis=0)
 
 
 def body(
@@ -280,13 +299,12 @@
     y, saved = forward(jnp.where(is_first, start, received), weights, tables)
     late = backward(last, saved, weights, tables, False)[0]
     received = lax.ppermute(late.astype(BF), "pipe", [(1, 0)])
-    dz, grad_qkv, grad_projt, small, grad_inner, grad_outert = backward(
+    dz, grad_qkv, grad_projt, small, rings = backward(
         jnp.where(is_first, received, last), saved, weights, tables, True
     )
-    outer_out = ring_scatter(grad_outert, False, STREAMS)
-    inner_out = ring_scatter(grad_inner, True, STREAMS)
+    outer_out, inner_out = (ring.finish() for ring in rings)
     packed_grads = jnp.concatenate(
-        [*grad_qkv, grad_projt, small.astype(BF),
+        [grad_qkv, grad_projt, small.astype(BF),
          jnp.zeros((features, 128 - small.shape[1]), BF)],
         axis=1,
     )

time: 675 us -> 694 us (1.028)
  waiting for transfers between devices: 234 us -> 256 us
    ppermute x28, waiting for transfers between devices: 104 us -> 125 us  [advance(): came = lax.ppermute(moving, 'dp', self.links).astype(F32)]
    dot_general x42 -> x40, matrix products: 113 us -> 119 us  [dot(): return jnp.einsum(spec, left, right, preferred_element_type=F32)]
    unnamed x130 -> x185, local copies, waits for them, and re-layouts: 25.8 us -> 23.4 us
  transfers between devices with their start and end apart: 63 -> 63, of which waited for: 32 -> 36; matrix products, arithmetic and copies ran while one was open for 31% -> 29% of each run, Pallas kernels for 0% -> 0%
where the time goes in v3:
time: 694 us; the launch traced here: 682 us
  waiting for transfers between devices  256 us (37%)
  matrix products  132 us (19%)
  local copies, waits for them, and re-layouts  129 us (19%)
  other arithmetic  62.8 us (9%)
  starting transfers between devices  55.9 us (8%)
  between operations  46.6 us (7%)
    ppermute x28, waiting for transfers between devices, advance(): came = lax.ppermute(moving, 'dp', self.links).astype(F32)  125 us
    dot_general x40, matrix products, dot(): return jnp.einsum(spec, left, right, preferred_element_type=F32)  119 us
    ppermute x14, waiting for transfers between devices, ring_gather(): moving = lax.ppermute(moving, 'dp', links)  98.1 us
    ppermute x28, starting transfers between devices, advance(): came = lax.ppermute(moving, 'dp', self.links).astype(F32)  33.6 us
    convert_element_type x24, other arithmetic, advance(): sums.append(total.astype(BF) if self.step < self.count else total)  33.2 us
    dynamic_update_slice x14, local copies, waits for them, and re-layouts, ring_gather(): whole = lax.dynamic_update_slice_in_dim(whole, moving, behind[step], 1)  29.7 us
    unnamed x185, local copies, waits for them, and re-layouts  23.4 us
    ppermute x14, starting transfers between devices, ring_gather(): moving = lax.ppermute(moving, 'dp', links)  15.5 us
  transfers between devices with their start and end apart: 63, of which 36 were waited for; matrix products, arithmetic and copies ran while one was open for 29% of the time, Pallas kernels for 0%

profile of v3, /device:TPU:0, one launch (start us, length us, event | category | flops | bytes accessed | tf_op | source)
XLA Modules:
  0.0 682.2 jit_solution(3916741699213583173)
XLA Ops:
  24.8 4.7 broadcast.206.clone
  30.7 22.9 %collective-permute-done.10 = bf16[4,1,96,1536]{3,2,0,1:T(8,128)(2,1)} collective-permute-done((bf16[4,1,96,1536]{3,2,0,1:T(8,128)(2,1)}, bf16[4,1,96,1536]{3,2,0,1:T(8,128)(2,1)}, u32[]{:S(2)}, u32[]{:S(2)}) %collective-permute-start.10) | collective-permute-done | bytes 1179680 | tf_op jit(solution)/shard_map/ppermute | solution.py:198
  93.3 8.3 %collective-permute-done.11 = bf16[4,1,96,1536]{3,2,0,1:T(8,128)(2,1)} collective-permute-done((bf16[4,1,96,1536]{3,2,0,1:T(8,128)(2,1)}, bf16[4,1,96,1536]{3,2,0,1:T(8,128)(2,1)}, u32[]{:S(2)}, u32[]{:S(2)}) %collective-permute-start.11) | collective-permute-done | bytes 1179680 | tf_op jit(solution)/shard_map/ppermute | solution.py:198
  109.5 19.7 %collective-permute-done.12 = bf16[4,1,96,1536]{3,2,0,1:T(8,128)(2,1)} collective-permute-done((bf16[4,1,96,1536]{3,2,0,1:T(8,128)(2,1)}, bf16[4,1,96,1536]{3,2,0,1:T(8,128)(2,1)}, u32[]{:S(2)}, u32[]{:S(2)}) %collective-permute-start.12) | collective-permute-done | bytes 1179680 | tf_op jit(solution)/shard_map/ppermute | solution.py:198
  146.5 9.5 %collective-permute-done.13 = bf16[4,1,96,1536]{3,2,0,1:T(8,128)(2,1)} collective-permute-done((bf16[4,1,96,1536]{3,2,0,1:T(8,128)(2,1)}, bf16[4,1,96,1536]{3,2,0,1:T(8,128)(2,1)}, u32[]{:S(2)}, u32[]{:S(2)}) %collective-permute-start.13) | collective-permute-done | bytes 1179680 | tf_op jit(solution)/shard_map/ppermute | solution.py:198
  176.3 5.9 collective-permute-done.14
  192.3 15.4 %collective-permute-done.15 = bf16[4,1,96,1536]{3,2,0,1:T(8,128)(2,1)} collective-permute-done((bf16[4,1,96,1536]{3,2,0,1:T(8,128)(2,1)}, bf16[4,1,96,1536]{3,2,0,1:T(8,128)(2,1)}, u32[]{:S(2)}, u32[]{:S(2)}) %collective-permute-start.15) | collective-permute-done | bytes 1179680 | tf_op jit(solution)/shard_map/ppermute | solution.py:198
  216.0 16.3 %collective-permute-done.16 = bf16[4,1,96,1536]{3,2,0,1:T(8,128)(2,1)S(1)} collective-permute-done((bf16[4,1,96,1536]{3,2,0,1:T(8,128)(2,1)}, bf16[4,1,96,1536]{3,2,0,1:T(8,128)(2,1)S(1)}, u32[]{:S(2)}, u32[]{:S(2)}) %collective-permute-start.16) | collective-permute-done | bytes 1179680 | tf_op jit(solution)/shard_map/ppermute | solution.py:198
  234.6 13.2 %fusion.26 = bf16[4,256,768]{2,1,0:T(8,128)(2,1)} fusion(bf16[4,768,1536]{2,1,0:T(8,128)(2,1)} %bitcast.69, bf16[4,256,768]{2,1,0:T(8,128)(2,1)} %bitcast.555, bf16[4,768,1536]{2,1,0:T(8,128)(2,1)} %bitcast.47), kind=kOutput, calls=%fused_computation.55 | convolution fusion | flops 4846780416 | bytes 22020096 | tf_op jit(solution)/shard_map/ecf,edf->ecd/dot_general | solution.py:18
  256.7 8.9 %collective-permute-done.18 = bf16[2,128,768]{2,1,0:T(8,128)(2,1)S(1)} collective-permute-done((bf16[2,128,768]{2,1,0:T(8,128)(2,1)}, bf16[2,128,768]{2,1,0:T(8,128)(2,1)S(1)}, u32[]{:S(2)}, u32[]{:S(2)}) %collective-permute-start.18) | collective-permute-done | bytes 393248 | tf_op jit(solution)/shard_map/ppermute | solution.py:298
  284.8 5.4 copy.626
  293.9 9.5 %fusion.187 = f32[4,256,1536]{2,1,0:T(8,128)} fusion(bf16[4,256,768]{1,2,0:T(8,128)(2,1)} %reshape.421, bf16[4,768,1536]{2,1,0:T(8,128)(2,1)} %bitcast.47), kind=kOutput, calls=%fused_computation.392 | convolution fusion | flops 2415919104 | bytes 17301504 | tf_op jit(solution)/shard_map/ecd,edf->ecf/dot_general | solution.py:18
  303.4 8.5 %convolution_convert_fusion.4 = bf16[4,256,768]{2,1,0:T(8,128)(2,1)S(1)} fusion(bf16[4,768,1536]{2,1,0:T(8,128)(2,1)} %bitcast.69, f32[4,256,1536]{2,1,0:T(8,128)} %fusion.187), kind=kOutput, calls=%fused_computation.58 | convolution fusion | flops 2430861312 | bytes 17301504 | tf_op jit(solution)/shard_map/ecf,edf->ecd/dot_general | solution.py:18
  321.7 12.9 %convolution_convert_fusion.3 = bf16[4,256,768]{2,1,0:T(8,128)(2,1)} fusion(bf16[4,768,1536]{2,1,0:T(8,128)(2,1)} %bitcast.47, bf16[4,256,768]{2,1,0:T(8,128)(2,1)} %bitcast.563, bf16[4,768,1536]{2,1,0:T(8,128)(2,1)} %bitcast.69, f32[4,256,1536]{2,1,0:T(8,128)} %fusion.187), kind=kOutput, calls=%fused_computation.57 | convolution fusion | flops 4862509056 | bytes 28311552 | tf_op jit(solution)/shard_map/ecf,edf->ecd/dot_general | solution.py:18
  358.2 11.9 %collective-permute-done.27 = bf16[2,128,768]{2,1,0:T(8,128)(2,1)S(1)} collective-permute-done((bf16[2,128,768]{2,1,0:T(8,128)(2,1)S(1)}, bf16[2,128,768]{2,1,0:T(8,128)(2,1)S(1)}, u32[]{:S(2)}, u32[]{:S(2)}) %collective-permute-start.27) | collective-permute-done | bytes 393248 | tf_op jit(solution)/shard_map/ppermute | solution.py:301
  383.9 9.7 %convolution_convert_fusion.1 = bf16[4,768,1536]{2,1,0:T(8,128)(2,1)} fusion(bf16[4,256,768]{2,1,0:T(8,128)(2,1)S(1)} %bitcast.556, f32[4,256,1536]{2,1,0:T(8,128)} %fusion.187), kind=kOutput, calls=%fused_computation.8 | convolution fusion | flops 2434793472 | bytes 17301504 | tf_op jit(solution)/shard_map/ecd,ecf->edf/dot_general | solution.py:18
  393.6 7.7 %multiply_convert_fusion = bf16[4,256,1536]{2,1,0:T(8,128)(2,1)S(1)} fusion(bf16[4,256,768]{2,1,0:T(8,128)(2,1)S(1)} %bitcast.557, bf16[4,768,1536]{2,1,0:T(8,128)(2,1)} %bitcast.69, f32[4,256,1536]{2,1,0:T(8,128)S(1)} %bitcast.537), kind=kOutput, calls=%fused_computation.20 | convolution fusion | flops 2445803520 | bytes 20447232 | tf_op jit(solution)/shard_map/ecd,edf->ecf/dot_general | solution.py:18
  401.3 5.1 convolution_convert_fusion
  406.4 6.4 convolution_convert_fusion.2
  416.4 6.5 fusion.173
  430.0 6.5 fusion.174
  446.4 8.6 %collective-permute-done.35 = bf16[2,96,1536]{2,1,0:T(8,128)(2,1)} collective-permute-done((bf16[2,96,1536]{2,1,0:T(8,128)(2,1)}, bf16[2,96,1536]{2,1,0:T(8,128)(2,1)}, u32[]{:S(2)}, u32[]{:S(2)}) %collective-permute-start.35) | collective-permute-done | bytes 589856 | tf_op jit(solution)/shard_map/ppermute | solution.py:221
  512.3 4.8 concatenate.60
  520.8 15.3 %collective-permute-done.46 = bf16[2,96,1536]{2,1,0:T(8,128)(2,1)} collective-permute-done((bf16[2,96,1536]{2,1,0:T(8,128)(2,1)}, bf16[2,96,1536]{2,1,0:T(8,128)(2,1)}, u32[]{:S(2)}, u32[]{:S(2)}) %collective-permute-start.46) | collective-permute-done | bytes 589856 | tf_op jit(solution)/shard_map/ppermute | solution.py:221
  544.8 16.6 %collective-permute-done.42 = bf16[2,96,1536]{2,1,0:T(8,128)(2,1)S(1)} collective-permute-done((bf16[2,96,1536]{2,1,0:T(8,128)(2,1)S(1)}, bf16[2,96,1536]{2,1,0:T(8,128)(2,1)S(1)}, u32[]{:S(2)}, u32[]{:S(2)}) %collective-permute-start.42) | collective-permute-done | bytes 589856 | tf_op jit(solution)/shard_map/ppermute | solution.py:221
  565.1 10.6 %collective-permute-done.47 = bf16[2,96,1536]{2,1,0:T(8,128)(2,1)S(1)} collective-permute-done((bf16[2,96,1536]{2,1,0:T(8,128)(2,1)S(1)}, bf16[2,96,1536]{2,1,0:T(8,128)(2,1)S(1)}, u32[]{:S(2)}, u32[]{:S(2)}) %collective-permute-start.47) | collective-permute-done | bytes 589856 | tf_op jit(solution)/shard_map/ppermute | solution.py:221
  581.7 6.5 collective-permute-done.43
  592.0 17.8 %collective-permute-done.48 = bf16[2,96,1536]{2,1,0:T(8,128)(2,1)S(1)} collective-permute-done((bf16[2,96,1536]{2,1,0:T(8,128)(2,1)S(1)}, bf16[2,96,1536]{2,1,0:T(8,128)(2,1)S(1)}, u32[]{:S(2)}, u32[]{:S(2)}) %collective-permute-start.48) | collective-permute-done | bytes 589856 | tf_op jit(solution)/shard_map/ppermute | solution.py:221
  614.8 4.9 collective-permute-done.58
  627.7 8.9 %collective-permute-done.49 = bf16[2,96,1536]{2,1,0:T(8,128)(2,1)S(1)} collective-permute-done((bf16[2,96,1536]{2,1,0:T(8,128)(2,1)S(1)}, bf16[2,96,1536]{2,1,0:T(8,128)(2,1)S(1)}, u32[]{:S(2)}, u32[]{:S(2)}) %collective-permute-start.49) | collective-permute-done | bytes 589856 | tf_op jit(solution)/shard_map/ppermute | solution.py:221
  643.6 5.7 collective-permute-done.45
  650.5 11.0 %collective-permute-done.50 = bf16[2,96,1536]{2,1,0:T(8,128)(2,1)S(1)} collective-permute-done((bf16[2,96,1536]{2,1,0:T(8,128)(2,1)S(1)}, bf16[2,96,1536]{2,1,0:T(8,128)(2,1)S(1)}, u32[]{:S(2)}, u32[]{:S(2)}) %collective-permute-start.50) | collective-permute-done | bytes 589856 | tf_op jit(solution)/shard_map/ppermute | solution.py:221
  (502 shorter events, 310.2 us)
Async XLA Ops:
  7.2 126.5 %all-gather.2.cloned.1.call-start = ((), (), s32[]{:S(2)}) async-start(), calls=%async_computation.1 | async-start | bytes 2875392 | tf_op jit(solution)/shard_map/all_gather | solution.py:170
  13.9 656.5 %reduce-scatter.2.cloned.1.call-start = ((), (), s32[]{:S(2)}) async-start(), calls=%async_computation.2 | async-start | bytes 2875392 | tf_op jit(solution)/shard_map/reduce_scatter | solution.py:174
  13.9 39.6 %collective-permute-start.10 = (bf16[4,1,96,1536]{3,2,0,1:T(8,128)(2,1)}, bf16[4,1,96,1536]{3,2,0,1:T(8,128)(2,1)}, u32[]{:S(2)}, u32[]{:S(2)}) collective-permute-start(bf16[4,1,96,1536]{3,2,0,1:T(8,128)(2,1)} %bitcast.568), channel_id=1, source_target_pairs={{1,3},{3,5},{5,7},{7,6},{6,4},{4,2},{2,0},{0,1},{9,11},{11,13},{13... | collective-permute-start | bytes 3538952 | tf_op jit(solution)/shard_map/ppermute | solution.py:198
  16.9 37.4 %collective-permute-start.3 = (bf16[4,1,96,1536]{3,2,0,1:T(8,128)(2,1)}, bf16[4,1,96,1536]{3,2,0,1:T(8,128)(2,1)S(1)}, u32[]{:S(2)}, u32[]{:S(2)}) collective-permute-start(bf16[4,1,96,1536]{3,2,0,1:T(8,128)(2,1)} %bitcast.569), channel_id=1, source_target_pairs={{0,2},{2,4},{4,6},{6,7},{7,5},{5,3},{3,1},{1,0},{8,10},{10,12},{12... | collective-permute-start | bytes 3538952 | tf_op jit(solution)/shard_map/ppermute | solution.py:198
  53.6 48.0 %collective-permute-start.11 = (bf16[4,1,96,1536]{3,2,0,1:T(8,128)(2,1)}, bf16[4,1,96,1536]{3,2,0,1:T(8,128)(2,1)}, u32[]{:S(2)}, u32[]{:S(2)}) collective-permute-start(bf16[4,1,96,1536]{3,2,0,1:T(8,128)(2,1)} %collective-permute-done.10), channel_id=1, source_target_pairs={{1,3},{3,5},{5,7},{7,6},{6,4},{4,2},{2,0},{0,1},{9,11},{11,13},{13... | collective-permute-start | bytes 3538952 | tf_op jit(solution)/shard_map/ppermute | solution.py:198
  54.3 47.3 %collective-permute-start.4 = (bf16[4,1,96,1536]{3,2,0,1:T(8,128)(2,1)S(1)}, bf16[4,1,96,1536]{3,2,0,1:T(8,128)(2,1)}, u32[]{:S(2)}, u32[]{:S(2)}) collective-permute-start(bf16[4,1,96,1536]{3,2,0,1:T(8,128)(2,1)S(1)} %collective-permute-done.3), channel_id=1, source_target_pairs={{0,2},{2,4},{4,6},{6,7},{7,5},{5,3},{3,1},{1,0},{8,10},{10,12},{12... | collective-permute-start | bytes 3538952 | tf_op jit(solution)/shard_map/ppermute | solution.py:198
  101.6 27.7 %collective-permute-start.12 = (bf16[4,1,96,1536]{3,2,0,1:T(8,128)(2,1)}, bf16[4,1,96,1536]{3,2,0,1:T(8,128)(2,1)}, u32[]{:S(2)}, u32[]{:S(2)}) collective-permute-start(bf16[4,1,96,1536]{3,2,0,1:T(8,128)(2,1)} %collective-permute-done.11), channel_id=1, source_target_pairs={{1,3},{3,5},{5,7},{7,6},{6,4},{4,2},{2,0},{0,1},{9,11},{11,13},{13... | collective-permute-start | bytes 3538952 | tf_op jit(solution)/shard_map/ppermute | solution.py:198
  101.6 28.0 %collective-permute-start.5 = (bf16[4,1,96,1536]{3,2,0,1:T(8,128)(2,1)}, bf16[4,1,96,1536]{3,2,0,1:T(8,128)(2,1)}, u32[]{:S(2)}, u32[]{:S(2)}) collective-permute-start(bf16[4,1,96,1536]{3,2,0,1:T(8,128)(2,1)} %collective-permute-done.4), channel_id=1, source_target_pairs={{0,2},{2,4},{4,6},{6,7},{7,5},{5,3},{3,1},{1,0},{8,10},{10,12},{12... | collective-permute-start | bytes 3538952 | tf_op jit(solution)/shard_map/ppermute | solution.py:198
  129.2 26.7 %collective-permute-start.13 = (bf16[4,1,96,1536]{3,2,0,1:T(8,128)(2,1)}, bf16[4,1,96,1536]{3,2,0,1:T(8,128)(2,1)}, u32[]{:S(2)}, u32[]{:S(2)}) collective-permute-start(bf16[4,1,96,1536]{3,2,0,1:T(8,128)(2,1)} %collective-permute-done.12), channel_id=1, source_target_pairs={{1,3},{3,5},{5,7},{7,6},{6,4},{4,2},{2,0},{0,1},{9,11},{11,13},{13... | collective-permute-start | bytes 3538952 | tf_op jit(solution)/shard_map/ppermute | solution.py:198
  129.6 27.0 %collective-permute-start.6 = (bf16[4,1,96,1536]{3,2,0,1:T(8,128)(2,1)}, bf16[4,1,96,1536]{3,2,0,1:T(8,128)(2,1)}, u32[]{:S(2)}, u32[]{:S(2)}) collective-permute-start(bf16[4,1,96,1536]{3,2,0,1:T(8,128)(2,1)} %collective-permute-done.5), channel_id=1, source_target_pairs={{0,2},{2,4},{4,6},{6,7},{7,5},{5,3},{3,1},{1,0},{8,10},{10,12},{12... | collective-permute-start | bytes 3538952 | tf_op jit(solution)/shard_map/ppermute | solution.py:198
  156.0 26.1 %collective-permute-start.14 = (bf16[4,1,96,1536]{3,2,0,1:T(8,128)(2,1)}, bf16[4,1,96,1536]{3,2,0,1:T(8,128)(2,1)}, u32[]{:S(2)}, u32[]{:S(2)}) collective-permute-start(bf16[4,1,96,1536]{3,2,0,1:T(8,128)(2,1)} %collective-permute-done.13), channel_id=1, source_target_pairs={{1,3},{3,5},{5,7},{7,6},{6,4},{4,2},{2,0},{0,1},{9,11},{11,13},{13... | collective-permute-start | bytes 3538952 | tf_op jit(solution)/shard_map/ppermute | solution.py:198
  156.6 26.1 %collective-permute-start.7 = (bf16[4,1,96,1536]{3,2,0,1:T(8,128)(2,1)}, bf16[4,1,96,1536]{3,2,0,1:T(8,128)(2,1)}, u32[]{:S(2)}, u32[]{:S(2)}) collective-permute-start(bf16[4,1,96,1536]{3,2,0,1:T(8,128)(2,1)} %collective-permute-done.6), channel_id=1, source_target_pairs={{0,2},{2,4},{4,6},{6,7},{7,5},{5,3},{3,1},{1,0},{8,10},{10,12},{12... | collective-permute-start | bytes 3538952 | tf_op jit(solution)/shard_map/ppermute | solution.py:198
  182.1 25.5 %collective-permute-start.15 = (bf16[4,1,96,1536]{3,2,0,1:T(8,128)(2,1)}, bf16[4,1,96,1536]{3,2,0,1:T(8,128)(2,1)}, u32[]{:S(2)}, u32[]{:S(2)}) collective-permute-start(bf16[4,1,96,1536]{3,2,0,1:T(8,128)(2,1)} %collective-permute-done.14), channel_id=1, source_target_pairs={{1,3},{3,5},{5,7},{7,6},{6,4},{4,2},{2,0},{0,1},{9,11},{11,13},{13... | collective-permute-start | bytes 3538952 | tf_op jit(solution)/shard_map/ppermute | solution.py:198
  182.7 27.4 %collective-permute-start.8 = (bf16[4,1,96,1536]{3,2,0,1:T(8,128)(2,1)}, bf16[4,1,96,1536]{3,2,0,1:T(8,128)(2,1)}, u32[]{:S(2)}, u32[]{:S(2)}) collective-permute-start(bf16[4,1,96,1536]{3,2,0,1:T(8,128)(2,1)} %collective-permute-done.7), channel_id=1, source_target_pairs={{0,2},{2,4},{4,6},{6,7},{7,5},{5,3},{3,1},{1,0},{8,10},{10,12},{12... | collective-permute-start | bytes 3538952 | tf_op jit(solution)/shard_map/ppermute | solution.py:198
  383.7 93.6 %collective-permute-start.22 = (f32[2,128,768]{2,1,0:T(8,128)}, f32[2,128,768]{2,1,0:T(8,128)}, u32[]{:S(2)}, u32[]{:S(2)}) collective-permute-start(f32[2,128,768]{2,1,0:T(8,128)} %get-tuple-element.144), channel_id=1, source_target_pairs={{0,8},{8,0},{1,9},{9,1},{2,10},{10,2},{3,11},{11,3},{4,12},{12,4},... | collective-permute-start | bytes 2359304 | tf_op jit(solution)/shard_map/ppermute | solution.py:22
  428.2 26.8 %collective-permute-start.35 = (bf16[2,96,1536]{2,1,0:T(8,128)(2,1)}, bf16[2,96,1536]{2,1,0:T(8,128)(2,1)}, u32[]{:S(2)}, u32[]{:S(2)}) collective-permute-start(bf16[2,96,1536]{2,1,0:T(8,128)(2,1)} %dynamic-slice_bitcast_fusion.1), channel_id=1, source_target_pairs={{0,2},{2,4},{4,6},{6,7},{7,5},{5,3},{3,1},{1,0},{8,10},{10,12},{12... | collective-permute-start | bytes 1769480 | tf_op jit(solution)/shard_map/ppermute | solution.py:221
  438.5 25.8 %collective-permute-start.31 = (bf16[2,96,1536]{2,1,0:T(8,128)(2,1)S(1)}, bf16[2,96,1536]{2,1,0:T(8,128)(2,1)S(1)}, u32[]{:S(2)}, u32[]{:S(2)}) collective-permute-start(bf16[2,96,1536]{2,1,0:T(8,128)(2,1)S(1)} %dynamic-slice_bitcast_fusion.3), channel_id=1, source_target_pairs={{1,3},{3,5},{5,7},{7,6},{6,4},{4,2},{2,0},{0,1},{9,11},{11,13},{13... | collective-permute-start | bytes 1769480 | tf_op jit(solution)/shard_map/ppermute | solution.py:221
  503.0 33.2 %collective-permute-start.46 = (bf16[2,96,1536]{2,1,0:T(8,128)(2,1)}, bf16[2,96,1536]{2,1,0:T(8,128)(2,1)}, u32[]{:S(2)}, u32[]{:S(2)}) collective-permute-start(bf16[2,96,1536]{2,1,0:T(8,128)(2,1)} %fusion.71), channel_id=1, source_target_pairs={{0,2},{2,4},{4,6},{6,7},{7,5},{5,3},{3,1},{1,0},{8,10},{10,12},{12... | collective-permute-start | bytes 1769480 | tf_op jit(solution)/shard_map/ppermute | solution.py:221
  504.3 35.8 %collective-permute-start.51 = (bf16[2,96,1536]{2,1,0:T(8,128)(2,1)}, bf16[2,96,1536]{2,1,0:T(8,128)(2,1)}, u32[]{:S(2)}, u32[]{:S(2)}) collective-permute-start(bf16[2,96,1536]{2,1,0:T(8,128)(2,1)} %fusion.77), channel_id=1, source_target_pairs={{1,3},{3,5},{5,7},{7,6},{6,4},{4,2},{2,0},{0,1},{9,11},{11,13},{13... | collective-permute-start | bytes 1769480 | tf_op jit(solution)/shard_map/ppermute | solution.py:221
  505.0 38.3 %collective-permute-start.56 = (bf16[2,96,1536]{2,1,0:T(8,128)(2,1)}, bf16[2,96,1536]{2,1,0:T(8,128)(2,1)}, u32[]{:S(2)}, u32[]{:S(2)}) collective-permute-start(bf16[2,96,1536]{2,1,0:T(8,128)(2,1)} %fusion.75), channel_id=1, source_target_pairs={{1,3},{3,5},{5,7},{7,6},{6,4},{4,2},{2,0},{0,1},{9,11},{11,13},{13... | collective-permute-start | bytes 1769480 | tf_op jit(solution)/shard_map/ppermute | solution.py:221
  519.1 42.3 %collective-permute-start.42 = (bf16[2,96,1536]{2,1,0:T(8,128)(2,1)S(1)}, bf16[2,96,1536]{2,1,0:T(8,128)(2,1)S(1)}, u32[]{:S(2)}, u32[]{:S(2)}) collective-permute-start(bf16[2,96,1536]{2,1,0:T(8,128)(2,1)S(1)} %fusion.70), channel_id=1, source_target_pairs={{0,2},{2,4},{4,6},{6,7},{7,5},{5,3},{3,1},{1,0},{8,10},{10,12},{12... | collective-permute-start | bytes 1769480 | tf_op jit(solution)/shard_map/ppermute | solution.py:221
  537.5 38.1 %collective-permute-start.47 = (bf16[2,96,1536]{2,1,0:T(8,128)(2,1)S(1)}, bf16[2,96,1536]{2,1,0:T(8,128)(2,1)S(1)}, u32[]{:S(2)}, u32[]{:S(2)}) collective-permute-start(bf16[2,96,1536]{2,1,0:T(8,128)(2,1)S(1)} %fusion.66), channel_id=1, source_target_pairs={{0,2},{2,4},{4,6},{6,7},{7,5},{5,3},{3,1},{1,0},{8,10},{10,12},{12... | collective-permute-start | bytes 1769480 | tf_op jit(solution)/shard_map/ppermute | solution.py:221
  541.5 37.9 %collective-permute-start.52 = (bf16[2,96,1536]{2,1,0:T(8,128)(2,1)S(1)}, bf16[2,96,1536]{2,1,0:T(8,128)(2,1)S(1)}, u32[]{:S(2)}, u32[]{:S(2)}) collective-permute-start(bf16[2,96,1536]{2,1,0:T(8,128)(2,1)S(1)} %fusion.62), channel_id=1, source_target_pairs={{1,3},{3,5},{5,7},{7,6},{6,4},{4,2},{2,0},{0,1},{9,11},{11,13},{13... | collective-permute-start | bytes 1769480 | tf_op jit(solution)/shard_map/ppermute | solution.py:221
  544.7 36.0 %collective-permute-start.57 = (bf16[2,96,1536]{2,1,0:T(8,128)(2,1)S(1)}, bf16[2,96,1536]{2,1,0:T(8,128)(2,1)S(1)}, u32[]{:S(2)}, u32[]{:S(2)}) collective-permute-start(bf16[2,96,1536]{2,1,0:T(8,128)(2,1)S(1)} %fusion.58), channel_id=1, source_target_pairs={{1,3},{3,5},{5,7},{7,6},{6,4},{4,2},{2,0},{0,1},{9,11},{11,13},{13... | collective-permute-start | bytes 1769480 | tf_op jit(solution)/shard_map/ppermute | solution.py:221
  562.5 25.7 %collective-permute-start.43 = (bf16[2,96,1536]{2,1,0:T(8,128)(2,1)S(1)}, bf16[2,96,1536]{2,1,0:T(8,128)(2,1)S(1)}, u32[]{:S(2)}, u32[]{:S(2)}) collective-permute-start(bf16[2,96,1536]{2,1,0:T(8,128)(2,1)S(1)} %fusion.69), channel_id=1, source_target_pairs={{0,2},{2,4},{4,6},{6,7},{7,5},{5,3},{3,1},{1,0},{8,10},{10,12},{12... | collective-permute-start | bytes 1769480 | tf_op jit(solution)/shard_map/ppermute | solution.py:221
  576.8 33.0 %collective-permute-start.48 = (bf16[2,96,1536]{2,1,0:T(8,128)(2,1)S(1)}, bf16[2,96,1536]{2,1,0:T(8,128)(2,1)S(1)}, u32[]{:S(2)}, u32[]{:S(2)}) collective-permute-start(bf16[2,96,1536]{2,1,0:T(8,128)(2,1)S(1)} %fusion.65), channel_id=1, source_target_pairs={{0,2},{2,4},{4,6},{6,7},{7,5},{5,3},{3,1},{1,0},{8,10},{10,12},{12... | collective-permute-start | bytes 1769480 | tf_op jit(solution)/shard_map/ppermute | solution.py:221
  580.6 32.9 %collective-permute-start.53 = (bf16[2,96,1536]{2,1,0:T(8,128)(2,1)S(1)}, bf16[2,96,1536]{2,1,0:T(8,128)(2,1)S(1)}, u32[]{:S(2)}, u32[]{:S(2)}) collective-permute-start(bf16[2,96,1536]{2,1,0:T(8,128)(2,1)S(1)} %fusion.61), channel_id=1, source_target_pairs={{1,3},{3,5},{5,7},{7,6},{6,4},{4,2},{2,0},{0,1},{9,11},{11,13},{13... | collective-permute-start | bytes 1769480 | tf_op jit(solution)/shard_map/ppermute | solution.py:221
  580.8 38.8 %collective-permute-start.58 = (bf16[2,96,1536]{2,1,0:T(8,128)(2,1)S(1)}, bf16[2,96,1536]{2,1,0:T(8,128)(2,1)S(1)}, u32[]{:S(2)}, u32[]{:S(2)}) collective-permute-start(bf16[2,96,1536]{2,1,0:T(8,128)(2,1)S(1)} %fusion.57), channel_id=1, source_target_pairs={{1,3},{3,5},{5,7},{7,6},{6,4},{4,2},{2,0},{0,1},{9,11},{11,13},{13... | collective-permute-start | bytes 1769480 | tf_op jit(solution)/shard_map/ppermute | solution.py:221
  589.5 34.5 %collective-permute-start.44 = (bf16[2,96,1536]{2,1,0:T(8,128)(2,1)S(1)}, bf16[2,96,1536]{2,1,0:T(8,128)(2,1)S(1)}, u32[]{:S(2)}, u32[]{:S(2)}) collective-permute-start(bf16[2,96,1536]{2,1,0:T(8,128)(2,1)S(1)} %fusion.68), channel_id=1, source_target_pairs={{0,2},{2,4},{4,6},{6,7},{7,5},{5,3},{3,1},{1,0},{8,10},{10,12},{12... | collective-permute-start | bytes 1769480 | tf_op jit(solution)/shard_map/ppermute | solution.py:221
  611.0 25.6 %collective-permute-start.49 = (bf16[2,96,1536]{2,1,0:T(8,128)(2,1)S(1)}, bf16[2,96,1536]{2,1,0:T(8,128)(2,1)S(1)}, u32[]{:S(2)}, u32[]{:S(2)}) collective-permute-start(bf16[2,96,1536]{2,1,0:T(8,128)(2,1)S(1)} %fusion.64), channel_id=1, source_target_pairs={{0,2},{2,4},{4,6},{6,7},{7,5},{5,3},{3,1},{1,0},{8,10},{10,12},{12... | collective-permute-start | bytes 1769480 | tf_op jit(solution)/shard_map/ppermute | solution.py:221
  614.7 25.6 %collective-permute-start.54 = (bf16[2,96,1536]{2,1,0:T(8,128)(2,1)S(1)}, bf16[2,96,1536]{2,1,0:T(8,128)(2,1)S(1)}, u32[]{:S(2)}, u32[]{:S(2)}) collective-permute-start(bf16[2,96,1536]{2,1,0:T(8,128)(2,1)S(1)} %fusion.60), channel_id=1, source_target_pairs={{1,3},{3,5},{5,7},{7,6},{6,4},{4,2},{2,0},{0,1},{9,11},{11,13},{13... | collective-permute-start | bytes 1769480 | tf_op jit(solution)/shard_map/ppermute | solution.py:221
  643.5 25.1 %collective-permute-start.60 = (bf16[2,96,1536]{2,1,0:T(8,128)(2,1)S(1)}, bf16[2,96,1536]{2,1,0:T(8,128)(2,1)S(1)}, u32[]{:S(2)}, u32[]{:S(2)}) collective-permute-start(bf16[2,96,1536]{2,1,0:T(8,128)(2,1)S(1)} %fusion.55), channel_id=1, source_target_pairs={{1,3},{3,5},{5,7},{7,6},{6,4},{4,2},{2,0},{0,1},{9,11},{11,13},{13... | collective-permute-start | bytes 1769480 | tf_op jit(solution)/shard_map/ppermute | solution.py:221
  (119 other events, 1759.9 us)
Sparse Core Ops, SparseCore 0:
  14.0 83.5 all-gather.1
  517.2 96.7 reduce-scatter.1
